TPU v7x, 32 devices: a whole 2x2x4 slice. The times are simulated.
32 devices in a mesh: rows: 8 (over z, x), cols: 4 (over y, core).
Axes of the slice: x: 2, y: 2, z: 4, core: 2. Of those that a mesh axis runs over, the one named last changes fastest.
Arguments:
- points: float32 [16, 32768], P(None, ('rows', 'cols')), may hold values from -6 to 6
- lengthscales: float32 [16], replicated, may hold values from 2 to 3
- targets: float32 [64, 32768], P(None, ('rows', 'cols')), may hold values from -6 to 6
- inducing_weights: bfloat16 [64, 2048], P(None, 'cols'), may hold values from -0.59765625 to 0.59765625
- inducing_index: int32 [2048], replicated, may hold values from 0 to 32767
- block_order: int32 [3], replicated, may hold values from 0 to 31
- block_inverse: bfloat16 [32, 1024, 1024], P(('rows', 'cols')), may hold values from -0.1 to 0.1
Outputs:
- residual: float32 [64, 32768], P(None, ('rows', 'cols'))
- weights: float32 [64, 32768], P(None, ('rows', 'cols'))
All inputs are finite; a program needn't handle non-finite values.
Results may differ from a plain program's by a relative error of at most 0.00095.
The roundings to bfloat16 on the way count: a program that leaves them out, or rounds other values in their place, can miss the bound.
Values may be sent and summed in bfloat16 or wider, within the bound.
No kernel may reach another device: no remote copies, remote signals or barrier semaphores. Data moves between devices by JAX's collectives and lax.ppermute only.
A program may use at most 64 MiB of HBM per device.

v0:
```python
import functools
import operator

import jax
import jax.numpy as jnp
from jax import lax
from jax.experimental import pallas as pl
from jax.experimental.pallas import tpu as pltpu
from jax.sharding import PartitionSpec as P


noise_var = 0.5
ALL = ("rows", "cols")
LANES = 128
UNIT = 4
PACK = 16
CHUNK = 512
WIDE = 256
LOG2_E = 1.4426950408889634
GRANT = 8 << 20


def exchange(value, mask):
    count = lax.axis_size(ALL)
    return lax.ppermute(value, ALL, [(i, i ^ mask) for i in range(count)])


def mask_groups():
    count = lax.axis_size(ALL)
    bits = [1 << k for k in range(1, count.bit_length() - 1)]
    return [bits[k : k + 2] for k in range(0, len(bits), 2)]


def choose_kernel(step_no, masks, device_ref, owners_ref, *refs):
    *options, out_ref = refs
    near = (device_ref[0] ^ owners_ref[step_no]) & functools.reduce(operator.or_, masks)
    for mask, option_ref in zip(masks, options):

        @pl.when(near == mask)
        def _():
            out_ref[...] = option_ref[...]


def spread_step(mine, other, step_no, device, owners):
    def choose(masks, options):
        (chosen,) = call(
            functools.partial(choose_kernel, step_no, tuple(masks)),
            [on_chip(mine.shape, mine.dtype)],
            [device, owners],
            options,
            [],
            1 << 10,
        )
        return chosen

    held = choose([0, 1], [mine, exchange(other, 1)])
    groups = mask_groups()
    for bits in groups:
        masks = [bits[0]] if len(bits) == 1 else [bits[0], bits[1], bits[0] | bits[1]]
        arrived = []
        for mask in masks:
            arrived.append(exchange(held, mask))
        held = choose([0, *masks], [held, *arrived])
    return held, exchange(held, 1)


def split3(value):
    high = value.astype(jnp.bfloat16)
    rest = value - high.astype(jnp.float32)
    middle = rest.astype(jnp.bfloat16)
    low = (rest - middle.astype(jnp.float32)).astype(jnp.bfloat16)
    return high, middle, low


def norm_rows(value, first):
    half = (-0.5 * LOG2_E) * jnp.sum(value * value, axis=0, keepdims=True)
    row = lax.broadcasted_iota(jnp.int32, (PACK, value.shape[1]), 0)
    block = jnp.where(row < 6, 1.0, 0.0)
    for k, part in enumerate(split3(half)):
        block = jnp.where(row == first + k, part.astype(jnp.float32), block)
    return block.astype(jnp.bfloat16)


def pack_left(value):
    high, middle, low = split3(value * LOG2_E)
    rows = [high, high, middle, high, low, middle, norm_rows(value, 0), jnp.zeros_like(high)]
    return jnp.concatenate(rows, axis=0)


def pack_right(value):
    high, middle, low = split3(value)
    rows = [high, middle, high, low, high, middle, norm_rows(value, 3), jnp.zeros_like(high)]
    return jnp.concatenate(rows, axis=0)


def kernel_values(left, right):
    exponent = jnp.dot(left, right, preferred_element_type=jnp.float32)
    return jnp.exp2(exponent).astype(jnp.bfloat16)


def units_of(rows, columns):
    return [(r, c) for r in range(0, rows, UNIT) for c in range(0, columns, LANES)]


def pick_kernel(per_anchor, device_ref, index_ref, points_ref, scale_ref, out_ref, scaled_ref):
    dims, points = points_ref.shape
    same = lax.broadcasted_iota(jnp.int32, (dims, dims), 0) == lax.broadcasted_iota(
        jnp.int32, (dims, dims), 1
    )
    scale = jnp.sum(jnp.where(same, scale_ref[...], 0.0), axis=1, keepdims=True)
    scaled = points_ref[...] / scale
    scaled_ref[...] = scaled
    count, per = out_ref.shape[:2]
    per_block = per - per_anchor
    anchors = index_ref.shape[1]
    anchor_units, block_units = units_of(dims, anchors), units_of(dims, points)
    if len(anchor_units) < count * per_anchor or len(block_units) < count * per_block:
        out_ref[...] = jnp.zeros_like(out_ref)
    for i, (r, c) in enumerate(block_units):
        out_ref[i // per_block, per_anchor + i % per_block] = scaled[r : r + UNIT, c : c + LANES]
    parts = jnp.concatenate(split3(scaled), axis=0)
    width = min(WIDE, anchors)
    place = {spot: i for i, spot in enumerate(anchor_units)}
    for start in range(0, anchors, width):
        local = index_ref[:, start : start + width] - device_ref[0] * points
        hot = lax.broadcasted_iota(jnp.int32, (points, width), 0) == local
        got = jnp.dot(parts, hot.astype(jnp.bfloat16), preferred_element_type=jnp.float32)
        got = (got[:dims] + got[dims : 2 * dims]) + got[2 * dims :]
        for r in range(0, dims, UNIT):
            for c in range(0, width, LANES):
                i = place[r, start + c]
                out_ref[i // per_anchor, i % per_anchor] = got[r : r + UNIT, c : c + LANES]


def merge_kernel(per_anchor, owners_ref, got_ref, out_ref):
    count, per = got_ref.shape[:2]
    per_block = per - per_anchor
    total = got_ref[0, :per_anchor]
    for source in range(1, count):
        total = total + got_ref[source, :per_anchor]
    pieces = [total]
    for k in range(owners_ref.shape[0]):
        pieces.append(got_ref[owners_ref[k], per_anchor : per_anchor + per_block])
    piece = jnp.concatenate(pieces, axis=0)
    for target in range(count):
        out_ref[target] = piece


def gather_units(got_ref, first, per, whole_ref):
    for i, (r, c) in enumerate(units_of(*whole_ref.shape)):
        whole_ref[r : r + UNIT, c : c + LANES] = got_ref[i // per, first + i % per]


def project(residual, slot, core, inverse_ref, whole_ref, mine_ref, other_ref):
    inverse = inverse_ref[slot]
    product = jnp.dot(residual.astype(jnp.bfloat16), inverse, preferred_element_type=jnp.float32)
    whole_ref[...] = product.astype(jnp.bfloat16)
    half = mine_ref.shape[0]
    mine_ref[...] = whole_ref[pl.ds(pl.multiple_of(core * half, half), half)]
    other_ref[...] = whole_ref[pl.ds(pl.multiple_of((1 - core) * half, half), half)]


def warm_kernel(per_anchor, device_ref, slots_ref, got_ref, scaled_ref, *refs):
    *weights, targets_ref, inverse_ref = refs[:-6]
    out_ref, mine_ref, other_ref, anchors_ref, left_ref, whole_ref = refs[-6:]
    gather_units(got_ref, 0, per_anchor, anchors_ref)
    left_ref[...] = pack_left(anchors_ref[...]).T
    right = pack_right(scaled_ref[...])
    column = lax.rem(device_ref[0], len(weights))
    share = weights[0].shape[1]
    step = min(CHUNK, share)
    for c in range(0, right.shape[1], WIDE):
        total = jnp.zeros((out_ref.shape[0], WIDE), jnp.float32)
        for mask, weights_ref in enumerate(weights):
            origin = (column ^ mask) * share
            for start in range(0, share, step):
                left = left_ref[pl.ds(pl.multiple_of(origin + start, LANES), step)]
                total = total + jnp.dot(
                    weights_ref[:, start : start + step],
                    kernel_values(left, right[:, c : c + WIDE]),
                    preferred_element_type=jnp.float32,
                )
        out_ref[:, c : c + WIDE] = targets_ref[:, c : c + WIDE] - total
    project(out_ref[...], slots_ref[0], device_ref[0] & 1, inverse_ref, whole_ref, mine_ref, other_ref)


def tile_kernel(first, per_block, got_ref, scaled_ref, out_ref, block_ref, left_ref):
    gather_units(got_ref, first, per_block, block_ref)
    left_ref[...] = pack_left(block_ref[...]).T
    right = pack_right(scaled_ref[...])
    for r in range(0, out_ref.shape[0], WIDE):
        for c in range(0, out_ref.shape[1], WIDE):
            out_ref[r : r + WIDE, c : c + WIDE] = kernel_values(
                left_ref[r : r + WIDE], right[:, c : c + WIDE]
            )


def update_kernel(step_no, last, device_ref, owners_ref, slots_ref, held_ref, partner_ref, tile_ref, *refs):
    half = held_ref.shape[0]
    core = device_ref[0] & 1
    if last:
        residual_ref, weights_ref, out_ref, sum_ref, whole_ref = refs
    else:
        residual_ref, weights_ref, inverse_ref = refs[:3]
        out_ref, sum_ref, mine_ref, other_ref, whole_ref = refs[3:]
    whole_ref[pl.ds(pl.multiple_of(core * half, half), half)] = held_ref[...]
    whole_ref[pl.ds(pl.multiple_of((1 - core) * half, half), half)] = partner_ref[...]
    delta = whole_ref[...]
    residual = residual_ref[...] - jnp.dot(
        delta, tile_ref[...], preferred_element_type=jnp.float32
    )
    owned = jnp.where(owners_ref[step_no] == device_ref[0], delta.astype(jnp.float32), 0.0)
    residual = residual - noise_var * owned
    out_ref[...] = residual
    sum_ref[...] = weights_ref[...] + owned
    if not last:
        project(residual, slots_ref[step_no + 1], core, inverse_ref, whole_ref, mine_ref, other_ref)


def on_chip(shape, dtype):
    return pltpu.VMEM(shape, dtype)


def call(kernel, out_shape, scalars, arrays, scratch, flops):
    memory = [pltpu.SMEM] * len(scalars) + [pltpu.VMEM] * len(arrays)
    return pl.pallas_call(
        kernel,
        out_shape=out_shape,
        in_specs=[pl.BlockSpec(memory_space=space) for space in memory],
        out_specs=[pl.BlockSpec(memory_space=pltpu.VMEM) for _ in out_shape],
        scratch_shapes=scratch,
        cost_estimate=pl.CostEstimate(flops=flops, transcendentals=0, bytes_accessed=1 << 20),
        compiler_params=pltpu.CompilerParams(vmem_limit_bytes=GRANT),
    )(*scalars, *[pltpu.with_memory_space_constraint(array, pltpu.VMEM) for array in arrays])


def body(
    points, lengthscales, targets, inducing_weights, inducing_index, block_order, block_inverse
):
    dims, points_dev = points.shape
    per_device = block_inverse.shape[0]
    step_count = block_order.shape[0]
    anchor_count = inducing_index.shape[0]
    count, col_count = lax.axis_size(ALL), lax.axis_size("cols")
    device = lax.axis_index(ALL).reshape(1)
    owners = block_order // per_device
    slots = block_order % per_device
    weights_of = [inducing_weights] + [
        lax.ppermute(inducing_weights, "cols", [(i, i ^ mask) for i in range(col_count)])
        for mask in range(1, col_count)
    ]
    per_anchor = -(-len(units_of(dims, anchor_count)) // count)
    per_block = -(-len(units_of(dims, points_dev)) // count)
    tile_flops = 2 * LANES * points_dev
    half = (targets.shape[0] // 2, points_dev)
    halves = [on_chip(half, jnp.bfloat16)] * 2
    out, scaled = call(
        functools.partial(pick_kernel, per_anchor),
        [
            on_chip((count, per_anchor + per_block, UNIT, LANES), jnp.float32),
            on_chip(points.shape, jnp.float32),
        ],
        [device],
        [inducing_index[None, :], points, lengthscales[None, :]],
        [],
        2 * 3 * dims * points_dev * anchor_count,
    )
    got = lax.all_to_all(out, ALL, 0, 0)
    (spread,) = call(
        functools.partial(merge_kernel, per_anchor),
        [on_chip((count, per_anchor + step_count * per_block, UNIT, LANES), jnp.float32)],
        [owners],
        [got],
        [],
        1 << 20,
    )
    got = lax.all_to_all(spread, ALL, 0, 0)
    residual, mine, other = call(
        functools.partial(warm_kernel, per_anchor),
        [on_chip(targets.shape, jnp.float32), *halves],
        [device, slots],
        [got, scaled, *weights_of, targets, block_inverse],
        [
            pltpu.VMEM((dims, anchor_count), jnp.float32),
            pltpu.VMEM((anchor_count, LANES), jnp.bfloat16),
            pltpu.VMEM(targets.shape, jnp.bfloat16),
        ],
        tile_flops * anchor_count,
    )
    weights = jnp.zeros_like(residual)
    for step_no in range(step_count):
        last = step_no == step_count - 1
        held, partner = spread_step(mine, other, step_no, device, owners)
        (tile,) = call(
            functools.partial(tile_kernel, per_anchor + step_no * per_block, per_block),
            [on_chip((points_dev, points_dev), jnp.bfloat16)],
            [],
            [got, scaled],
            [pltpu.VMEM(points.shape, jnp.float32), pltpu.VMEM((points_dev, LANES), jnp.bfloat16)],
            tile_flops * points_dev,
        )
        state = [held, partner, tile, residual, weights]
        shape = jax.ShapeDtypeStruct if last else on_chip
        results = call(
            functools.partial(update_kernel, step_no, last),
            [shape(targets.shape, jnp.float32)] * 2 + ([] if last else halves),
            [device, owners, slots],
            state if last else state + [block_inverse],
            [pltpu.VMEM(targets.shape, jnp.bfloat16)],
            tile_flops * points_dev // 4,
        )
        residual, weights = results[:2]
        mine, other = results[2:] if not last else (None, None)
    return (residual, weights)


def solution(mesh):
    placed = (
        P(None, ALL),
        P(),
        P(None, ALL),
        P(None, "cols"),
        P(),
        P(),
        P(ALL, None, None),
    )

    return jax.shard_map(
        body,
        mesh=mesh,
        in_specs=placed,
        out_specs=(P(None, ALL), P(None, ALL)),
        check_vma=False,
    )
```

profile of v0, /device:TPU:0, one launch (start us, length us, event | category | flops | bytes accessed | tf_op | source)
XLA Modules:
  0.0 106.7 jit_solution(662610681711255598)
XLA Ops:
  0.7 1.0 copy-done.5
  1.6 0.7 copy-done.6
  2.3 0.7 copy-done.7
  3.0 0.9 shard_map.86
  3.9 16.1 %all_to_all.10.got_ref = f32[32,3,4,128]{3,2,1,0:T(4,128)S(1)} all-to-all(f32[32,3,4,128]{3,2,1,0:T(4,128)S(1)} %get-tuple-element.15), channel_id=1, replica_groups=mesh['rows'=8,'cols'=4] {'rows','cols'}, dimensions={0} | all-to-all | bytes 393216 | tf_op jit(solution)/shard_map/all_to_all | solution.py:268
  20.0 0.7 copy-done.2
  20.7 1.3 %shard_map.87 = f32[32,5,4,128]{3,2,1,0:T(4,128)} custom-call(s32[3]{0:T(128)S(1)} %copy-done.2, f32[32,3,4,128]{3,2,1,0:T(4,128)S(1)} %all_to_all.10.got_ref), custom_call_target="tpu_custom_call" | custom-call | flops 1048576 | bytes 1048576 | tf_op jit(solution)/shard_map/pallas_call | solution.py:226
  22.0 2.6 %all-to-all-start.1 = ((f32[32,5,4,128]{3,2,1,0:T(4,128)}), f32[32,5,4,128]{3,2,1,0:T(4,128)S(1)}, u32[]{:S(2)}, u32[]{:S(2)}) async-start(f32[32,5,4,128]{3,2,1,0:T(4,128)} %shard_map.87), calls=%async_computation.1 | async-start | bytes 655360 | tf_op jit(solution)/shard_map/all_to_all | solution.py:277
  24.9 1.6 %collective-permute-start.1 = (bf16[64,512]{1,0:T(8,128)(2,1)}, bf16[64,512]{1,0:T(8,128)(2,1)S(1)}, u32[]{:S(2)}, u32[]{:S(2)}) collective-permute-start(bf16[64,512]{1,0:T(8,128)(2,1)} %refs_0_.1), channel_id=1, source_target_pairs={{0,2},{1,3},{2,0},{3,1},{4,6},{5,7},{6,4},{7,5},{8,10},{9,11},{10,... | collective-permute-start | bytes 196616 | tf_op jit(solution)/shard_map/ppermute | solution.py:249
  26.6 5.5 %collective-permute-done.1.refs_2_ = bf16[64,512]{1,0:T(8,128)(2,1)S(1)} collective-permute-done((bf16[64,512]{1,0:T(8,128)(2,1)}, bf16[64,512]{1,0:T(8,128)(2,1)S(1)}, u32[]{:S(2)}, u32[]{:S(2)}) %collective-permute-start.1) | collective-permute-done | bytes 65568 | tf_op jit(solution)/shard_map/ppermute | solution.py:249
  32.0 0.8 collective-permute-done.2.refs_3_
  32.8 3.8 %all-to-all-done.1.got_ref = f32[32,5,4,128]{3,2,1,0:T(4,128)S(1)} async-done(((f32[32,5,4,128]{3,2,1,0:T(4,128)}), f32[32,5,4,128]{3,2,1,0:T(4,128)S(1)}, u32[]{:S(2)}, u32[]{:S(2)}) %all-to-all-start.1) | async-done | bytes 327712 | tf_op jit(solution)/shard_map/all_to_all | solution.py:277
  36.7 0.9 copy-done.1
  37.6 0.8 copy-done.4
  38.5 3.5 %shard_map.88 = (f32[64,1024]{1,0:T(8,128)S(1)}, bf16[32,1024]{1,0:T(8,128)(2,1)S(1)}, bf16[32,1024]{1,0:T(8,128)(2,1)S(1)}) custom-call(s32[1]{0:T(128)} %bitcast.device_ref, s32[3]{0:T(128)S(1)} %ne.14.slots_ref, f32[32,5,4,128]{3,2,1,0:T(4,128)S(1)} %all-to-all-done.1.got_ref, f32[16,1024]{1,0:T(8,128)S(1)} %get-tuple-element.16.scaled_ref, ...), custom_call_target="tpu_custom_call" | custom-call | flops 536870912 | bytes 1048576 | tf_op jit(solution)/shard_map/pallas_call | solution.py:226
  42.1 1.2 %collective-permute-done.3.refs_1_ = bf16[32,1024]{1,0:T(8,128)(2,1)S(1)} collective-permute-done((bf16[32,1024]{1,0:T(8,128)(2,1)S(1)}, bf16[32,1024]{1,0:T(8,128)(2,1)S(1)}, u32[]{:S(2)}, u32[]{:S(2)}) %collective-permute-start.3) | collective-permute-done | bytes 65568 | tf_op jit(solution)/shard_map/ppermute | solution.py:25
  43.3 0.6 shard_map.89.refs_0_
  44.3 1.3 %collective-permute-start.5 = (bf16[32,1024]{1,0:T(8,128)(2,1)S(1)}, bf16[32,1024]{1,0:T(8,128)(2,1)S(1)}, u32[]{:S(2)}, u32[]{:S(2)}) collective-permute-start(bf16[32,1024]{1,0:T(8,128)(2,1)S(1)} %shard_map.89.refs_0_), channel_id=1, source_target_pairs={{0,4},{1,5},{2,6},{3,7},{4,0},{5,1},{6,2},{7,3},{8,12},{9,13},{10,... | collective-permute-start | bytes 196616 | tf_op jit(solution)/shard_map/ppermute | solution.py:25
  45.6 1.8 %collective-permute-start.6 = (bf16[32,1024]{1,0:T(8,128)(2,1)S(1)}, bf16[32,1024]{1,0:T(8,128)(2,1)S(1)}, u32[]{:S(2)}, u32[]{:S(2)}) collective-permute-start(bf16[32,1024]{1,0:T(8,128)(2,1)S(1)} %shard_map.89.refs_0_), channel_id=1, source_target_pairs={{0,6},{1,7},{2,4},{3,5},{4,2},{5,3},{6,0},{7,1},{8,14},{9,15},{10,... | collective-permute-start | bytes 196616 | tf_op jit(solution)/shard_map/ppermute | solution.py:25
  47.4 0.8 collective-permute-done.4.refs_1_
  48.2 0.6 collective-permute-done.5.refs_2_
  48.8 2.0 %collective-permute-done.6.refs_3_ = bf16[32,1024]{1,0:T(8,128)(2,1)S(1)} collective-permute-done((bf16[32,1024]{1,0:T(8,128)(2,1)S(1)}, bf16[32,1024]{1,0:T(8,128)(2,1)S(1)}, u32[]{:S(2)}, u32[]{:S(2)}) %collective-permute-start.6) | collective-permute-done | bytes 65568 | tf_op jit(solution)/shard_map/ppermute | solution.py:25
  50.8 0.6 shard_map.90.refs_0_
  51.4 0.7 collective-permute-start.7
  52.1 1.3 %collective-permute-start.8 = (bf16[32,1024]{1,0:T(8,128)(2,1)S(1)}, bf16[32,1024]{1,0:T(8,128)(2,1)S(1)}, u32[]{:S(2)}, u32[]{:S(2)}) collective-permute-start(bf16[32,1024]{1,0:T(8,128)(2,1)S(1)} %shard_map.90.refs_0_), channel_id=1, source_target_pairs={{0,16},{1,17},{2,18},{3,19},{4,20},{5,21},{6,22},{7,23},{8,24},{9,... | collective-permute-start | bytes 196616 | tf_op jit(solution)/shard_map/ppermute | solution.py:25
  53.4 2.4 %collective-permute-start.9 = (bf16[32,1024]{1,0:T(8,128)(2,1)S(1)}, bf16[32,1024]{1,0:T(8,128)(2,1)S(1)}, u32[]{:S(2)}, u32[]{:S(2)}) collective-permute-start(bf16[32,1024]{1,0:T(8,128)(2,1)S(1)} %shard_map.90.refs_0_), channel_id=1, source_target_pairs={{0,24},{1,25},{2,26},{3,27},{4,28},{5,29},{6,30},{7,31},{8,16},{9,... | collective-permute-start | bytes 196616 | tf_op jit(solution)/shard_map/ppermute | solution.py:25
  55.9 2.6 %collective-permute-done.8.refs_2_ = bf16[32,1024]{1,0:T(8,128)(2,1)S(1)} collective-permute-done((bf16[32,1024]{1,0:T(8,128)(2,1)S(1)}, bf16[32,1024]{1,0:T(8,128)(2,1)S(1)}, u32[]{:S(2)}, u32[]{:S(2)}) %collective-permute-start.8) | collective-permute-done | bytes 65568 | tf_op jit(solution)/shard_map/ppermute | solution.py:25
  58.5 1.1 %collective-permute-done.9.refs_3_ = bf16[32,1024]{1,0:T(8,128)(2,1)S(1)} collective-permute-done((bf16[32,1024]{1,0:T(8,128)(2,1)S(1)}, bf16[32,1024]{1,0:T(8,128)(2,1)S(1)}, u32[]{:S(2)}, u32[]{:S(2)}) %collective-permute-start.9) | collective-permute-done | bytes 65568 | tf_op jit(solution)/shard_map/ppermute | solution.py:25
  59.6 0.6 shard_map.91.held_ref
  60.2 0.8 shard_map.92.tile_ref
  61.5 1.4 %shard_map.93 = (f32[64,1024]{1,0:T(8,128)S(1)}, f32[64,1024]{1,0:T(8,128)S(1)}, bf16[32,1024]{1,0:T(8,128)(2,1)S(1)}, bf16[32,1024]{1,0:T(8,128)(2,1)S(1)}) custom-call(s32[1]{0:T(128)} %bitcast.device_ref, s32[3]{0:T(128)S(1)} %copy-done.3, s32[3]{0:T(128)S(1)} %ne.14.slots_ref, bf16[32,1024]{1,0:T(8,128)(2,1)S(1)} %shard_map.91.held_ref, ...), custom_call_target="tpu_custom_call" | custom-call | flops 67108864 | bytes 1048576 | tf_op jit(solution)/shard_map/pallas_call | solution.py:226
  63.2 1.1 %collective-permute-done.11.refs_1_ = bf16[32,1024]{1,0:T(8,128)(2,1)S(1)} collective-permute-done((bf16[32,1024]{1,0:T(8,128)(2,1)S(1)}, bf16[32,1024]{1,0:T(8,128)(2,1)S(1)}, u32[]{:S(2)}, u32[]{:S(2)}) %collective-permute-start.11) | collective-permute-done | bytes 65568 | tf_op jit(solution)/shard_map/ppermute | solution.py:25
  64.2 0.6 shard_map.94.refs_0_
  64.8 0.8 collective-permute-start.12
  65.6 1.2 %collective-permute-start.13 = (bf16[32,1024]{1,0:T(8,128)(2,1)S(1)}, bf16[32,1024]{1,0:T(8,128)(2,1)S(1)}, u32[]{:S(2)}, u32[]{:S(2)}) collective-permute-start(bf16[32,1024]{1,0:T(8,128)(2,1)S(1)} %shard_map.94.refs_0_), channel_id=1, source_target_pairs={{0,4},{1,5},{2,6},{3,7},{4,0},{5,1},{6,2},{7,3},{8,12},{9,13},{10,... | collective-permute-start | bytes 196616 | tf_op jit(solution)/shard_map/ppermute | solution.py:25
  66.8 1.5 %collective-permute-start.14 = (bf16[32,1024]{1,0:T(8,128)(2,1)S(1)}, bf16[32,1024]{1,0:T(8,128)(2,1)S(1)}, u32[]{:S(2)}, u32[]{:S(2)}) collective-permute-start(bf16[32,1024]{1,0:T(8,128)(2,1)S(1)} %shard_map.94.refs_0_), channel_id=1, source_target_pairs={{0,6},{1,7},{2,4},{3,5},{4,2},{5,3},{6,0},{7,1},{8,14},{9,15},{10,... | collective-permute-start | bytes 196616 | tf_op jit(solution)/shard_map/ppermute | solution.py:25
  68.4 0.8 collective-permute-done.12.refs_1_
  69.1 1.3 %collective-permute-done.13.refs_2_ = bf16[32,1024]{1,0:T(8,128)(2,1)S(1)} collective-permute-done((bf16[32,1024]{1,0:T(8,128)(2,1)S(1)}, bf16[32,1024]{1,0:T(8,128)(2,1)S(1)}, u32[]{:S(2)}, u32[]{:S(2)}) %collective-permute-start.13) | collective-permute-done | bytes 65568 | tf_op jit(solution)/shard_map/ppermute | solution.py:25
  70.4 1.6 %collective-permute-done.14.refs_3_ = bf16[32,1024]{1,0:T(8,128)(2,1)S(1)} collective-permute-done((bf16[32,1024]{1,0:T(8,128)(2,1)S(1)}, bf16[32,1024]{1,0:T(8,128)(2,1)S(1)}, u32[]{:S(2)}, u32[]{:S(2)}) %collective-permute-start.14) | collective-permute-done | bytes 65568 | tf_op jit(solution)/shard_map/ppermute | solution.py:25
  72.0 0.6 shard_map.95.refs_0_
  72.6 1.2 %collective-permute-start.15 = (bf16[32,1024]{1,0:T(8,128)(2,1)S(1)}, bf16[32,1024]{1,0:T(8,128)(2,1)S(1)}, u32[]{:S(2)}, u32[]{:S(2)}) collective-permute-start(bf16[32,1024]{1,0:T(8,128)(2,1)S(1)} %shard_map.95.refs_0_), channel_id=1, source_target_pairs={{0,8},{1,9},{2,10},{3,11},{4,12},{5,13},{6,14},{7,15},{8,0},{9,1},... | collective-permute-start | bytes 196616 | tf_op jit(solution)/shard_map/ppermute | solution.py:25
  73.8 2.1 %collective-permute-start.16 = (bf16[32,1024]{1,0:T(8,128)(2,1)S(1)}, bf16[32,1024]{1,0:T(8,128)(2,1)S(1)}, u32[]{:S(2)}, u32[]{:S(2)}) collective-permute-start(bf16[32,1024]{1,0:T(8,128)(2,1)S(1)} %shard_map.95.refs_0_), channel_id=1, source_target_pairs={{0,16},{1,17},{2,18},{3,19},{4,20},{5,21},{6,22},{7,23},{8,24},{9,... | collective-permute-start | bytes 196616 | tf_op jit(solution)/shard_map/ppermute | solution.py:25
  75.9 1.1 %collective-permute-start.17 = (bf16[32,1024]{1,0:T(8,128)(2,1)S(1)}, bf16[32,1024]{1,0:T(8,128)(2,1)S(1)}, u32[]{:S(2)}, u32[]{:S(2)}) collective-permute-start(bf16[32,1024]{1,0:T(8,128)(2,1)S(1)} %shard_map.95.refs_0_), channel_id=1, source_target_pairs={{0,24},{1,25},{2,26},{3,27},{4,28},{5,29},{6,30},{7,31},{8,16},{9,... | collective-permute-start | bytes 196616 | tf_op jit(solution)/shard_map/ppermute | solution.py:25
  77.2 3.1 %collective-permute-done.16.refs_2_ = bf16[32,1024]{1,0:T(8,128)(2,1)S(1)} collective-permute-done((bf16[32,1024]{1,0:T(8,128)(2,1)S(1)}, bf16[32,1024]{1,0:T(8,128)(2,1)S(1)}, u32[]{:S(2)}, u32[]{:S(2)}) %collective-permute-start.16) | collective-permute-done | bytes 65568 | tf_op jit(solution)/shard_map/ppermute | solution.py:25
  80.3 1.6 %collective-permute-done.17.refs_3_ = bf16[32,1024]{1,0:T(8,128)(2,1)S(1)} collective-permute-done((bf16[32,1024]{1,0:T(8,128)(2,1)S(1)}, bf16[32,1024]{1,0:T(8,128)(2,1)S(1)}, u32[]{:S(2)}, u32[]{:S(2)}) %collective-permute-start.17) | collective-permute-done | bytes 65568 | tf_op jit(solution)/shard_map/ppermute | solution.py:25
  82.0 0.6 shard_map.96.held_ref
  82.6 0.8 shard_map.97.tile_ref
  83.9 1.4 %shard_map.98 = (f32[64,1024]{1,0:T(8,128)S(1)}, f32[64,1024]{1,0:T(8,128)S(1)}, bf16[32,1024]{1,0:T(8,128)(2,1)S(1)}, bf16[32,1024]{1,0:T(8,128)(2,1)S(1)}) custom-call(s32[1]{0:T(128)} %bitcast.device_ref, s32[3]{0:T(128)S(1)} %copy-done.3, s32[3]{0:T(128)S(1)} %ne.14.slots_ref, bf16[32,1024]{1,0:T(8,128)(2,1)S(1)} %shard_map.96.held_ref, ...), custom_call_target="tpu_custom_call" | custom-call | flops 67108864 | bytes 1048576 | tf_op jit(solution)/shard_map/pallas_call | solution.py:226
  85.5 1.1 %collective-permute-done.19.refs_1_ = bf16[32,1024]{1,0:T(8,128)(2,1)S(1)} collective-permute-done((bf16[32,1024]{1,0:T(8,128)(2,1)S(1)}, bf16[32,1024]{1,0:T(8,128)(2,1)S(1)}, u32[]{:S(2)}, u32[]{:S(2)}) %collective-permute-start.19) | collective-permute-done | bytes 65568 | tf_op jit(solution)/shard_map/ppermute | solution.py:25
  86.6 0.6 shard_map.99.refs_0_
  87.2 0.7 collective-permute-start.20
  87.9 1.1 %collective-permute-start.21 = (bf16[32,1024]{1,0:T(8,128)(2,1)S(1)}, bf16[32,1024]{1,0:T(8,128)(2,1)S(1)}, u32[]{:S(2)}, u32[]{:S(2)}) collective-permute-start(bf16[32,1024]{1,0:T(8,128)(2,1)S(1)} %shard_map.99.refs_0_), channel_id=1, source_target_pairs={{0,4},{1,5},{2,6},{3,7},{4,0},{5,1},{6,2},{7,3},{8,12},{9,13},{10,... | collective-permute-start | bytes 196616 | tf_op jit(solution)/shard_map/ppermute | solution.py:25
  89.0 1.7 %collective-permute-start.22 = (bf16[32,1024]{1,0:T(8,128)(2,1)S(1)}, bf16[32,1024]{1,0:T(8,128)(2,1)S(1)}, u32[]{:S(2)}, u32[]{:S(2)}) collective-permute-start(bf16[32,1024]{1,0:T(8,128)(2,1)S(1)} %shard_map.99.refs_0_), channel_id=1, source_target_pairs={{0,6},{1,7},{2,4},{3,5},{4,2},{5,3},{6,0},{7,1},{8,14},{9,15},{10,... | collective-permute-start | bytes 196616 | tf_op jit(solution)/shard_map/ppermute | solution.py:25
  90.7 0.8 collective-permute-done.20.refs_1_
  91.5 1.1 %collective-permute-done.21.refs_2_ = bf16[32,1024]{1,0:T(8,128)(2,1)S(1)} collective-permute-done((bf16[32,1024]{1,0:T(8,128)(2,1)S(1)}, bf16[32,1024]{1,0:T(8,128)(2,1)S(1)}, u32[]{:S(2)}, u32[]{:S(2)}) %collective-permute-start.21) | collective-permute-done | bytes 65568 | tf_op jit(solution)/shard_map/ppermute | solution.py:25
  92.6 1.6 %collective-permute-done.22.refs_3_ = bf16[32,1024]{1,0:T(8,128)(2,1)S(1)} collective-permute-done((bf16[32,1024]{1,0:T(8,128)(2,1)S(1)}, bf16[32,1024]{1,0:T(8,128)(2,1)S(1)}, u32[]{:S(2)}, u32[]{:S(2)}) %collective-permute-start.22) | collective-permute-done | bytes 65568 | tf_op jit(solution)/shard_map/ppermute | solution.py:25
  94.2 0.6 shard_map.100.refs_0_
  94.8 2.1 %collective-permute-start.24 = (bf16[32,1024]{1,0:T(8,128)(2,1)S(1)}, bf16[32,1024]{1,0:T(8,128)(2,1)S(1)}, u32[]{:S(2)}, u32[]{:S(2)}) collective-permute-start(bf16[32,1024]{1,0:T(8,128)(2,1)S(1)} %shard_map.100.refs_0_), channel_id=1, source_target_pairs={{0,16},{1,17},{2,18},{3,19},{4,20},{5,21},{6,22},{7,23},{8,24},{9,... | collective-permute-start | bytes 196616 | tf_op jit(solution)/shard_map/ppermute | solution.py:25
  96.9 2.3 %collective-permute-start.25 = (bf16[32,1024]{1,0:T(8,128)(2,1)S(1)}, bf16[32,1024]{1,0:T(8,128)(2,1)S(1)}, u32[]{:S(2)}, u32[]{:S(2)}) collective-permute-start(bf16[32,1024]{1,0:T(8,128)(2,1)S(1)} %shard_map.100.refs_0_), channel_id=1, source_target_pairs={{0,24},{1,25},{2,26},{3,27},{4,28},{5,29},{6,30},{7,31},{8,16},{9,... | collective-permute-start | bytes 196616 | tf_op jit(solution)/shard_map/ppermute | solution.py:25
  99.2 2.4 %collective-permute-done.24.refs_2_ = bf16[32,1024]{1,0:T(8,128)(2,1)S(1)} collective-permute-done((bf16[32,1024]{1,0:T(8,128)(2,1)S(1)}, bf16[32,1024]{1,0:T(8,128)(2,1)S(1)}, u32[]{:S(2)}, u32[]{:S(2)}) %collective-permute-start.24) | collective-permute-done | bytes 65568 | tf_op jit(solution)/shard_map/ppermute | solution.py:25
  101.7 1.4 %collective-permute-done.25.refs_3_ = bf16[32,1024]{1,0:T(8,128)(2,1)S(1)} collective-permute-done((bf16[32,1024]{1,0:T(8,128)(2,1)S(1)}, bf16[32,1024]{1,0:T(8,128)(2,1)S(1)}, u32[]{:S(2)}, u32[]{:S(2)}) %collective-permute-start.25) | collective-permute-done | bytes 65568 | tf_op jit(solution)/shard_map/ppermute | solution.py:25
  103.1 0.6 shard_map.101.held_ref
  103.7 0.8 shard_map.102.tile_ref
  105.0 1.7 %shard_map.103 = (f32[64,1024]{1,0:T(8,128)}, f32[64,1024]{1,0:T(8,128)}) custom-call(s32[1]{0:T(128)} %bitcast.device_ref, s32[3]{0:T(128)S(1)} %copy-done.3, s32[3]{0:T(128)S(1)} %ne.14.slots_ref, bf16[32,1024]{1,0:T(8,128)(2,1)S(1)} %shard_map.101.held_ref, bf16[32,1024]{1,0:T(8,128)(2,1)S(1)} %collective-permute-done.26.partner_ref, ...), custom_call_target="tpu_custom_call" | custom-call | flops 67108864 | bytes 1048576 | tf_op jit(solution)/shard_map/pallas_call | solution.py:226
  (29 shorter events, 3.2 us)
Async XLA Ops:
  0.6 36.0 %copy-start = (bf16[1,1024,1024]{2,1,0:T(8,128)(2,1)S(1)}, bf16[1,1024,1024]{2,1,0:T(8,128)(2,1)}, u32[]{:S(2)}) copy-start(bf16[1,1024,1024]{2,1,0:T(8,128)(2,1)} %refs_2_.3) | copy-start | bytes 6291460
  0.6 1.0 copy-start.5
  1.6 0.7 copy-start.6
  2.3 0.7 copy-start.7
  20.0 0.7 copy-start.2
  20.7 22.7 %copy-start.3 = (s32[3]{0:T(128)S(1)}, s32[3]{0:T(128)}, u32[]{:S(2)}) copy-start(s32[3]{0:T(128)} %owners_ref.12) | copy-start | bytes 40
  22.0 14.7 %all-to-all-start.1 = ((f32[32,5,4,128]{3,2,1,0:T(4,128)}), f32[32,5,4,128]{3,2,1,0:T(4,128)S(1)}, u32[]{:S(2)}, u32[]{:S(2)}) async-start(f32[32,5,4,128]{3,2,1,0:T(4,128)} %shard_map.87), calls=%async_computation.1 | async-start | bytes 655360 | tf_op jit(solution)/shard_map/all_to_all | solution.py:277
  24.6 2.0 %collective-permute-start = (bf16[64,512]{1,0:T(8,128)(2,1)}, bf16[64,512]{1,0:T(8,128)(2,1)S(1)}, u32[]{:S(2)}, u32[]{:S(2)}) collective-permute-start(bf16[64,512]{1,0:T(8,128)(2,1)} %refs_0_.1), channel_id=1, source_target_pairs={{0,1},{1,0},{2,3},{3,2},{4,5},{5,4},{6,7},{7,6},{8,9},{9,8},{10,11... | collective-permute-start | bytes 196616 | tf_op jit(solution)/shard_map/ppermute | solution.py:249
  24.9 7.1 %collective-permute-start.1 = (bf16[64,512]{1,0:T(8,128)(2,1)}, bf16[64,512]{1,0:T(8,128)(2,1)S(1)}, u32[]{:S(2)}, u32[]{:S(2)}) collective-permute-start(bf16[64,512]{1,0:T(8,128)(2,1)} %refs_0_.1), channel_id=1, source_target_pairs={{0,2},{1,3},{2,0},{3,1},{4,6},{5,7},{6,4},{7,5},{8,10},{9,11},{10,... | collective-permute-start | bytes 196616 | tf_op jit(solution)/shard_map/ppermute | solution.py:249
  26.6 6.2 %collective-permute-start.2 = (bf16[64,512]{1,0:T(8,128)(2,1)}, bf16[64,512]{1,0:T(8,128)(2,1)S(1)}, u32[]{:S(2)}, u32[]{:S(2)}) collective-permute-start(bf16[64,512]{1,0:T(8,128)(2,1)} %refs_0_.1), channel_id=1, source_target_pairs={{0,3},{1,2},{2,1},{3,0},{4,7},{5,6},{6,5},{7,4},{8,11},{9,10},{10,... | collective-permute-start | bytes 196616 | tf_op jit(solution)/shard_map/ppermute | solution.py:249
  36.7 1.0 copy-start.1
  37.6 0.8 copy-start.4
  42.0 1.3 %collective-permute-start.3 = (bf16[32,1024]{1,0:T(8,128)(2,1)S(1)}, bf16[32,1024]{1,0:T(8,128)(2,1)S(1)}, u32[]{:S(2)}, u32[]{:S(2)}) collective-permute-start(bf16[32,1024]{1,0:T(8,128)(2,1)S(1)} %get-tuple-element.18), channel_id=1, source_target_pairs={{0,1},{1,0},{2,3},{3,2},{4,5},{5,4},{6,7},{7,6},{8,9},{9,8},{10,11... | collective-permute-start | bytes 196616 | tf_op jit(solution)/shard_map/ppermute | solution.py:25
  43.9 4.3 %collective-permute-start.4 = (bf16[32,1024]{1,0:T(8,128)(2,1)S(1)}, bf16[32,1024]{1,0:T(8,128)(2,1)S(1)}, u32[]{:S(2)}, u32[]{:S(2)}) collective-permute-start(bf16[32,1024]{1,0:T(8,128)(2,1)S(1)} %shard_map.89.refs_0_), channel_id=1, source_target_pairs={{0,2},{1,3},{2,0},{3,1},{4,6},{5,7},{6,4},{7,5},{8,10},{9,11},{10,... | collective-permute-start | bytes 196616 | tf_op jit(solution)/shard_map/ppermute | solution.py:25
  44.3 4.5 %collective-permute-start.5 = (bf16[32,1024]{1,0:T(8,128)(2,1)S(1)}, bf16[32,1024]{1,0:T(8,128)(2,1)S(1)}, u32[]{:S(2)}, u32[]{:S(2)}) collective-permute-start(bf16[32,1024]{1,0:T(8,128)(2,1)S(1)} %shard_map.89.refs_0_), channel_id=1, source_target_pairs={{0,4},{1,5},{2,6},{3,7},{4,0},{5,1},{6,2},{7,3},{8,12},{9,13},{10,... | collective-permute-start | bytes 196616 | tf_op jit(solution)/shard_map/ppermute | solution.py:25
  45.6 5.2 %collective-permute-start.6 = (bf16[32,1024]{1,0:T(8,128)(2,1)S(1)}, bf16[32,1024]{1,0:T(8,128)(2,1)S(1)}, u32[]{:S(2)}, u32[]{:S(2)}) collective-permute-start(bf16[32,1024]{1,0:T(8,128)(2,1)S(1)} %shard_map.89.refs_0_), channel_id=1, source_target_pairs={{0,6},{1,7},{2,4},{3,5},{4,2},{5,3},{6,0},{7,1},{8,14},{9,15},{10,... | collective-permute-start | bytes 196616 | tf_op jit(solution)/shard_map/ppermute | solution.py:25
  51.4 4.5 %collective-permute-start.7 = (bf16[32,1024]{1,0:T(8,128)(2,1)S(1)}, bf16[32,1024]{1,0:T(8,128)(2,1)S(1)}, u32[]{:S(2)}, u32[]{:S(2)}) collective-permute-start(bf16[32,1024]{1,0:T(8,128)(2,1)S(1)} %shard_map.90.refs_0_), channel_id=1, source_target_pairs={{0,8},{1,9},{2,10},{3,11},{4,12},{5,13},{6,14},{7,15},{8,0},{9,1},... | collective-permute-start | bytes 196616 | tf_op jit(solution)/shard_map/ppermute | solution.py:25
  52.1 6.3 %collective-permute-start.8 = (bf16[32,1024]{1,0:T(8,128)(2,1)S(1)}, bf16[32,1024]{1,0:T(8,128)(2,1)S(1)}, u32[]{:S(2)}, u32[]{:S(2)}) collective-permute-start(bf16[32,1024]{1,0:T(8,128)(2,1)S(1)} %shard_map.90.refs_0_), channel_id=1, source_target_pairs={{0,16},{1,17},{2,18},{3,19},{4,20},{5,21},{6,22},{7,23},{8,24},{9,... | collective-permute-start | bytes 196616 | tf_op jit(solution)/shard_map/ppermute | solution.py:25
  53.4 6.2 %collective-permute-start.9 = (bf16[32,1024]{1,0:T(8,128)(2,1)S(1)}, bf16[32,1024]{1,0:T(8,128)(2,1)S(1)}, u32[]{:S(2)}, u32[]{:S(2)}) collective-permute-start(bf16[32,1024]{1,0:T(8,128)(2,1)S(1)} %shard_map.90.refs_0_), channel_id=1, source_target_pairs={{0,24},{1,25},{2,26},{3,27},{4,28},{5,29},{6,30},{7,31},{8,16},{9,... | collective-permute-start | bytes 196616 | tf_op jit(solution)/shard_map/ppermute | solution.py:25
  60.2 1.3 %collective-permute-start.10 = (bf16[32,1024]{1,0:T(8,128)(2,1)S(1)}, bf16[32,1024]{1,0:T(8,128)(2,1)S(1)}, u32[]{:S(2)}, u32[]{:S(2)}) collective-permute-start(bf16[32,1024]{1,0:T(8,128)(2,1)S(1)} %shard_map.91.held_ref), channel_id=1, source_target_pairs={{0,1},{1,0},{2,3},{3,2},{4,5},{5,4},{6,7},{7,6},{8,9},{9,8},{10,11... | collective-permute-start | bytes 196616 | tf_op jit(solution)/shard_map/ppermute | solution.py:25
  62.9 1.3 %collective-permute-start.11 = (bf16[32,1024]{1,0:T(8,128)(2,1)S(1)}, bf16[32,1024]{1,0:T(8,128)(2,1)S(1)}, u32[]{:S(2)}, u32[]{:S(2)}) collective-permute-start(bf16[32,1024]{1,0:T(8,128)(2,1)S(1)} %get-tuple-element.21), channel_id=1, source_target_pairs={{0,1},{1,0},{2,3},{3,2},{4,5},{5,4},{6,7},{7,6},{8,9},{9,8},{10,11... | collective-permute-start | bytes 196616 | tf_op jit(solution)/shard_map/ppermute | solution.py:25
  64.8 4.3 %collective-permute-start.12 = (bf16[32,1024]{1,0:T(8,128)(2,1)S(1)}, bf16[32,1024]{1,0:T(8,128)(2,1)S(1)}, u32[]{:S(2)}, u32[]{:S(2)}) collective-permute-start(bf16[32,1024]{1,0:T(8,128)(2,1)S(1)} %shard_map.94.refs_0_), channel_id=1, source_target_pairs={{0,2},{1,3},{2,0},{3,1},{4,6},{5,7},{6,4},{7,5},{8,10},{9,11},{10,... | collective-permute-start | bytes 196616 | tf_op jit(solution)/shard_map/ppermute | solution.py:25
  65.6 4.9 %collective-permute-start.13 = (bf16[32,1024]{1,0:T(8,128)(2,1)S(1)}, bf16[32,1024]{1,0:T(8,128)(2,1)S(1)}, u32[]{:S(2)}, u32[]{:S(2)}) collective-permute-start(bf16[32,1024]{1,0:T(8,128)(2,1)S(1)} %shard_map.94.refs_0_), channel_id=1, source_target_pairs={{0,4},{1,5},{2,6},{3,7},{4,0},{5,1},{6,2},{7,3},{8,12},{9,13},{10,... | collective-permute-start | bytes 196616 | tf_op jit(solution)/shard_map/ppermute | solution.py:25
  66.8 5.2 %collective-permute-start.14 = (bf16[32,1024]{1,0:T(8,128)(2,1)S(1)}, bf16[32,1024]{1,0:T(8,128)(2,1)S(1)}, u32[]{:S(2)}, u32[]{:S(2)}) collective-permute-start(bf16[32,1024]{1,0:T(8,128)(2,1)S(1)} %shard_map.94.refs_0_), channel_id=1, source_target_pairs={{0,6},{1,7},{2,4},{3,5},{4,2},{5,3},{6,0},{7,1},{8,14},{9,15},{10,... | collective-permute-start | bytes 196616 | tf_op jit(solution)/shard_map/ppermute | solution.py:25
  72.6 4.7 %collective-permute-start.15 = (bf16[32,1024]{1,0:T(8,128)(2,1)S(1)}, bf16[32,1024]{1,0:T(8,128)(2,1)S(1)}, u32[]{:S(2)}, u32[]{:S(2)}) collective-permute-start(bf16[32,1024]{1,0:T(8,128)(2,1)S(1)} %shard_map.95.refs_0_), channel_id=1, source_target_pairs={{0,8},{1,9},{2,10},{3,11},{4,12},{5,13},{6,14},{7,15},{8,0},{9,1},... | collective-permute-start | bytes 196616 | tf_op jit(solution)/shard_map/ppermute | solution.py:25
  73.8 6.6 %collective-permute-start.16 = (bf16[32,1024]{1,0:T(8,128)(2,1)S(1)}, bf16[32,1024]{1,0:T(8,128)(2,1)S(1)}, u32[]{:S(2)}, u32[]{:S(2)}) collective-permute-start(bf16[32,1024]{1,0:T(8,128)(2,1)S(1)} %shard_map.95.refs_0_), channel_id=1, source_target_pairs={{0,16},{1,17},{2,18},{3,19},{4,20},{5,21},{6,22},{7,23},{8,24},{9,... | collective-permute-start | bytes 196616 | tf_op jit(solution)/shard_map/ppermute | solution.py:25
  75.9 6.1 %collective-permute-start.17 = (bf16[32,1024]{1,0:T(8,128)(2,1)S(1)}, bf16[32,1024]{1,0:T(8,128)(2,1)S(1)}, u32[]{:S(2)}, u32[]{:S(2)}) collective-permute-start(bf16[32,1024]{1,0:T(8,128)(2,1)S(1)} %shard_map.95.refs_0_), channel_id=1, source_target_pairs={{0,24},{1,25},{2,26},{3,27},{4,28},{5,29},{6,30},{7,31},{8,16},{9,... | collective-permute-start | bytes 196616 | tf_op jit(solution)/shard_map/ppermute | solution.py:25
  82.6 1.3 %collective-permute-start.18 = (bf16[32,1024]{1,0:T(8,128)(2,1)S(1)}, bf16[32,1024]{1,0:T(8,128)(2,1)S(1)}, u32[]{:S(2)}, u32[]{:S(2)}) collective-permute-start(bf16[32,1024]{1,0:T(8,128)(2,1)S(1)} %shard_map.96.held_ref), channel_id=1, source_target_pairs={{0,1},{1,0},{2,3},{3,2},{4,5},{5,4},{6,7},{7,6},{8,9},{9,8},{10,11... | collective-permute-start | bytes 196616 | tf_op jit(solution)/shard_map/ppermute | solution.py:25
  85.3 1.3 %collective-permute-start.19 = (bf16[32,1024]{1,0:T(8,128)(2,1)S(1)}, bf16[32,1024]{1,0:T(8,128)(2,1)S(1)}, u32[]{:S(2)}, u32[]{:S(2)}) collective-permute-start(bf16[32,1024]{1,0:T(8,128)(2,1)S(1)} %get-tuple-element.25), channel_id=1, source_target_pairs={{0,1},{1,0},{2,3},{3,2},{4,5},{5,4},{6,7},{7,6},{8,9},{9,8},{10,11... | collective-permute-start | bytes 196616 | tf_op jit(solution)/shard_map/ppermute | solution.py:25
  87.2 4.3 %collective-permute-start.20 = (bf16[32,1024]{1,0:T(8,128)(2,1)S(1)}, bf16[32,1024]{1,0:T(8,128)(2,1)S(1)}, u32[]{:S(2)}, u32[]{:S(2)}) collective-permute-start(bf16[32,1024]{1,0:T(8,128)(2,1)S(1)} %shard_map.99.refs_0_), channel_id=1, source_target_pairs={{0,2},{1,3},{2,0},{3,1},{4,6},{5,7},{6,4},{7,5},{8,10},{9,11},{10,... | collective-permute-start | bytes 196616 | tf_op jit(solution)/shard_map/ppermute | solution.py:25
  87.9 4.7 %collective-permute-start.21 = (bf16[32,1024]{1,0:T(8,128)(2,1)S(1)}, bf16[32,1024]{1,0:T(8,128)(2,1)S(1)}, u32[]{:S(2)}, u32[]{:S(2)}) collective-permute-start(bf16[32,1024]{1,0:T(8,128)(2,1)S(1)} %shard_map.99.refs_0_), channel_id=1, source_target_pairs={{0,4},{1,5},{2,6},{3,7},{4,0},{5,1},{6,2},{7,3},{8,12},{9,13},{10,... | collective-permute-start | bytes 196616 | tf_op jit(solution)/shard_map/ppermute | solution.py:25
  89.0 5.2 %collective-permute-start.22 = (bf16[32,1024]{1,0:T(8,128)(2,1)S(1)}, bf16[32,1024]{1,0:T(8,128)(2,1)S(1)}, u32[]{:S(2)}, u32[]{:S(2)}) collective-permute-start(bf16[32,1024]{1,0:T(8,128)(2,1)S(1)} %shard_map.99.refs_0_), channel_id=1, source_target_pairs={{0,6},{1,7},{2,4},{3,5},{4,2},{5,3},{6,0},{7,1},{8,14},{9,15},{10,... | collective-permute-start | bytes 196616 | tf_op jit(solution)/shard_map/ppermute | solution.py:25
  94.8 4.5 %collective-permute-start.23 = (bf16[32,1024]{1,0:T(8,128)(2,1)S(1)}, bf16[32,1024]{1,0:T(8,128)(2,1)S(1)}, u32[]{:S(2)}, u32[]{:S(2)}) collective-permute-start(bf16[32,1024]{1,0:T(8,128)(2,1)S(1)} %shard_map.100.refs_0_), channel_id=1, source_target_pairs={{0,8},{1,9},{2,10},{3,11},{4,12},{5,13},{6,14},{7,15},{8,0},{9,1},... | collective-permute-start | bytes 196616 | tf_op jit(solution)/shard_map/ppermute | solution.py:25
  94.8 6.8 %collective-permute-start.24 = (bf16[32,1024]{1,0:T(8,128)(2,1)S(1)}, bf16[32,1024]{1,0:T(8,128)(2,1)S(1)}, u32[]{:S(2)}, u32[]{:S(2)}) collective-permute-start(bf16[32,1024]{1,0:T(8,128)(2,1)S(1)} %shard_map.100.refs_0_), channel_id=1, source_target_pairs={{0,16},{1,17},{2,18},{3,19},{4,20},{5,21},{6,22},{7,23},{8,24},{9,... | collective-permute-start | bytes 196616 | tf_op jit(solution)/shard_map/ppermute | solution.py:25
  96.9 6.2 %collective-permute-start.25 = (bf16[32,1024]{1,0:T(8,128)(2,1)S(1)}, bf16[32,1024]{1,0:T(8,128)(2,1)S(1)}, u32[]{:S(2)}, u32[]{:S(2)}) collective-permute-start(bf16[32,1024]{1,0:T(8,128)(2,1)S(1)} %shard_map.100.refs_0_), channel_id=1, source_target_pairs={{0,24},{1,25},{2,26},{3,27},{4,28},{5,29},{6,30},{7,31},{8,16},{9,... | collective-permute-start | bytes 196616 | tf_op jit(solution)/shard_map/ppermute | solution.py:25
  103.6 1.3 %collective-permute-start.26 = (bf16[32,1024]{1,0:T(8,128)(2,1)S(1)}, bf16[32,1024]{1,0:T(8,128)(2,1)S(1)}, u32[]{:S(2)}, u32[]{:S(2)}) collective-permute-start(bf16[32,1024]{1,0:T(8,128)(2,1)S(1)} %shard_map.101.held_ref), channel_id=1, source_target_pairs={{0,1},{1,0},{2,3},{3,2},{4,5},{5,4},{6,7},{7,6},{8,9},{9,8},{10,11... | collective-permute-start | bytes 196616 | tf_op jit(solution)/shard_map/ppermute | solution.py:25
where the time goes:
time: 107 us
  waiting for transfers between devices  37.9 us (35%)
  starting transfers between devices  29.3 us (27%)
  Pallas kernels  17.7 us (17%)
  blocking collectives  16.1 us (15%)
  local copies, waits for them, and re-layouts  4.8 us (4%)
    ppermute x24, waiting for transfers between devices, exchange(): return lax.ppermute(value, ALL, [(i, i ^ mask) for i in range(count)])  27.8 us
    ppermute x24, starting transfers between devices, exchange(): return lax.ppermute(value, ALL, [(i, i ^ mask) for i in range(count)])  24.7 us
    pallas_call x18, Pallas kernels, call(): pl.pallas_call(kernel, out_shape=out_shape, in_specs=[pl.BlockSpec(memory...  17.7 us
    all_to_all x1, blocking collectives, body(): got = lax.all_to_all(out, ALL, 0, 0)  16.1 us
    ppermute x3, waiting for transfers between devices, body(): lax.ppermute(inducing_weights, 'cols', [(i, i ^ mask) for i in range(col_...  6.25 us
    unnamed x16, local copies, waits for them, and re-layouts  4.78 us
    all_to_all x1, waiting for transfers between devices, body(): got = lax.all_to_all(spread, ALL, 0, 0)  3.84 us
    all_to_all x1, starting transfers between devices, body(): got = lax.all_to_all(spread, ALL, 0, 0)  2.62 us
  transfers between devices with their start and end apart: 28, of which 25 were waited for; matrix products, arithmetic and copies ran while one was open for 0% of the time, Pallas kernels for 2%

commit v1 on v0

--- a/solution.py
+++ b/solution.py
@@ -31,9 +31,13 @@
     return [bits[k : k + 2] for k in range(0, len(bits), 2)]
 
 
-def choose_kernel(step_no, masks, device_ref, owners_ref, *refs):
+def scalar(table_ref, row):
+    return table_ref[row][0, 0]
+
+
+def choose_kernel(step_no, masks, table_ref, *refs):
     *options, out_ref = refs
-    near = (device_ref[0] ^ owners_ref[step_no]) & functools.reduce(operator.or_, masks)
+    near = scalar(table_ref, 1 + step_no) & functools.reduce(operator.or_, masks)
     for mask, option_ref in zip(masks, options):
 
         @pl.when(near == mask)
@@ -41,13 +45,13 @@
             out_ref[...] = option_ref[...]
 
 
-def spread_step(mine, other, step_no, device, owners):
+def spread_step(mine, other, step_no, table):
     def choose(masks, options):
         (chosen,) = call(
             functools.partial(choose_kernel, step_no, tuple(masks)),
             [on_chip(mine.shape, mine.dtype)],
-            [device, owners],
-            options,
+            [],
+            placed_on_chip([table, *options]),
             [],
             1 << 10,
         )
@@ -102,8 +106,17 @@
     return [(r, c) for r in range(0, rows, UNIT) for c in range(0, columns, LANES)]
 
 
-def pick_kernel(per_anchor, device_ref, index_ref, points_ref, scale_ref, out_ref, scaled_ref):
+def pick_kernel(
+    per_anchor, device_ref, owners_ref, slots_ref, index_ref, points_ref, scale_ref, out_ref,
+    scaled_ref, table_ref,
+):
     dims, points = points_ref.shape
+    device = device_ref[0]
+    steps = owners_ref.shape[0]
+    table_ref[0] = jnp.full(table_ref.shape[1:], device, jnp.int32)
+    for k in range(steps):
+        table_ref[1 + k] = jnp.full(table_ref.shape[1:], device ^ owners_ref[k], jnp.int32)
+        table_ref[1 + steps + k] = jnp.full(table_ref.shape[1:], slots_ref[k], jnp.int32)
     same = lax.broadcasted_iota(jnp.int32, (dims, dims), 0) == lax.broadcasted_iota(
         jnp.int32, (dims, dims), 1
     )
@@ -122,7 +135,7 @@
     width = min(WIDE, anchors)
     place = {spot: i for i, spot in enumerate(anchor_units)}
     for start in range(0, anchors, width):
-        local = index_ref[:, start : start + width] - device_ref[0] * points
+        local = index_ref[:, start : start + width] - device * points
         hot = lax.broadcasted_iota(jnp.int32, (points, width), 0) == local
         got = jnp.dot(parts, hot.astype(jnp.bfloat16), preferred_element_type=jnp.float32)
         got = (got[:dims] + got[dims : 2 * dims]) + got[2 * dims :]
@@ -132,15 +145,18 @@
                 out_ref[i // per_anchor, i % per_anchor] = got[r : r + UNIT, c : c + LANES]
 
 
-def merge_kernel(per_anchor, owners_ref, got_ref, out_ref):
+def merge_kernel(per_anchor, steps, table_ref, got_ref, *refs):
+    out_ref = refs[-1]
     count, per = got_ref.shape[:2]
     per_block = per - per_anchor
+    device = scalar(table_ref, 0)
     total = got_ref[0, :per_anchor]
     for source in range(1, count):
         total = total + got_ref[source, :per_anchor]
     pieces = [total]
-    for k in range(owners_ref.shape[0]):
-        pieces.append(got_ref[owners_ref[k], per_anchor : per_anchor + per_block])
+    for k in range(steps):
+        owner = scalar(table_ref, 1 + k) ^ device
+        pieces.append(got_ref[owner, per_anchor : per_anchor + per_block])
     piece = jnp.concatenate(pieces, axis=0)
     for target in range(count):
         out_ref[target] = piece
@@ -160,28 +176,37 @@
     other_ref[...] = whole_ref[pl.ds(pl.multiple_of((1 - core) * half, half), half)]
 
 
-def warm_kernel(per_anchor, device_ref, slots_ref, got_ref, scaled_ref, *refs):
-    *weights, targets_ref, inverse_ref = refs[:-6]
-    out_ref, mine_ref, other_ref, anchors_ref, left_ref, whole_ref = refs[-6:]
+def warm_kernel(per_anchor, steps, table_ref, got_ref, scaled_ref, inverse_ref, *refs):
+    *shares, aim_ref = refs[:-9]
+    out_ref, mine_ref, other_ref, anchors_ref, left_ref, whole_ref = refs[-9:-3]
+    share_ref, targets_ref, sems = refs[-3:]
+    fetches = [pltpu.make_async_copy(aim_ref, targets_ref, sems.at[len(shares)])]
+    for i, ref in enumerate(shares):
+        fetches.append(pltpu.make_async_copy(ref, share_ref.at[i], sems.at[i]))
+    for fetch in fetches:
+        fetch.start()
+    device = scalar(table_ref, 0)
     gather_units(got_ref, 0, per_anchor, anchors_ref)
     left_ref[...] = pack_left(anchors_ref[...]).T
     right = pack_right(scaled_ref[...])
-    column = lax.rem(device_ref[0], len(weights))
-    share = weights[0].shape[1]
+    column = lax.rem(device, len(shares))
+    for fetch in fetches:
+        fetch.wait()
+    share = share_ref.shape[2]
     step = min(CHUNK, share)
     for c in range(0, right.shape[1], WIDE):
         total = jnp.zeros((out_ref.shape[0], WIDE), jnp.float32)
-        for mask, weights_ref in enumerate(weights):
+        for mask in range(len(shares)):
             origin = (column ^ mask) * share
             for start in range(0, share, step):
                 left = left_ref[pl.ds(pl.multiple_of(origin + start, LANES), step)]
                 total = total + jnp.dot(
-                    weights_ref[:, start : start + step],
+                    share_ref[mask, :, start : start + step],
                     kernel_values(left, right[:, c : c + WIDE]),
                     preferred_element_type=jnp.float32,
                 )
         out_ref[:, c : c + WIDE] = targets_ref[:, c : c + WIDE] - total
-    project(out_ref[...], slots_ref[0], device_ref[0] & 1, inverse_ref, whole_ref, mine_ref, other_ref)
+    project(out_ref[...], scalar(table_ref, 1 + steps), device & 1, inverse_ref, whole_ref, mine_ref, other_ref)
 
 
 def tile_kernel(first, per_block, got_ref, scaled_ref, out_ref, block_ref, left_ref):
@@ -195,34 +220,36 @@
             )
 
 
-def update_kernel(step_no, last, device_ref, owners_ref, slots_ref, held_ref, partner_ref, tile_ref, *refs):
+def update_kernel(step_no, steps, table_ref, held_ref, partner_ref, tile_ref, *refs):
     half = held_ref.shape[0]
-    core = device_ref[0] & 1
-    if last:
-        residual_ref, weights_ref, out_ref, sum_ref, whole_ref = refs
-    else:
-        residual_ref, weights_ref, inverse_ref = refs[:3]
-        out_ref, sum_ref, mine_ref, other_ref, whole_ref = refs[3:]
+    device = scalar(table_ref, 0)
+    core = device & 1
+    refs = list(refs)
+    residual_ref = refs.pop(0)
+    weights_ref = refs.pop(0) if step_no else None
+    inverse_ref = refs.pop(0) if step_no < steps - 1 else None
+    out_ref, sum_ref, *halves, whole_ref = refs
     whole_ref[pl.ds(pl.multiple_of(core * half, half), half)] = held_ref[...]
     whole_ref[pl.ds(pl.multiple_of((1 - core) * half, half), half)] = partner_ref[...]
     delta = whole_ref[...]
     residual = residual_ref[...] - jnp.dot(
         delta, tile_ref[...], preferred_element_type=jnp.float32
     )
-    owned = jnp.where(owners_ref[step_no] == device_ref[0], delta.astype(jnp.float32), 0.0)
+    owned = jnp.where(scalar(table_ref, 1 + step_no) == 0, delta.astype(jnp.float32), 0.0)
     residual = residual - noise_var * owned
     out_ref[...] = residual
-    sum_ref[...] = weights_ref[...] + owned
-    if not last:
-        project(residual, slots_ref[step_no + 1], core, inverse_ref, whole_ref, mine_ref, other_ref)
+    sum_ref[...] = weights_ref[...] + owned if step_no else owned
+    if step_no < steps - 1:
+        slot = scalar(table_ref, 2 + steps + step_no)
+        project(residual, slot, core, inverse_ref, whole_ref, *halves)
 
 
 def on_chip(shape, dtype):
     return pltpu.VMEM(shape, dtype)
 
 
-def call(kernel, out_shape, scalars, arrays, scratch, flops):
-    memory = [pltpu.SMEM] * len(scalars) + [pltpu.VMEM] * len(arrays)
+def call(kernel, out_shape, scalars, arrays, scratch, flops, outside=()):
+    memory = [pltpu.SMEM] * len(scalars) + [pltpu.VMEM] * len(arrays) + [pltpu.HBM] * len(outside)
     return pl.pallas_call(
         kernel,
         out_shape=out_shape,
@@ -231,7 +258,15 @@
         scratch_shapes=scratch,
         cost_estimate=pl.CostEstimate(flops=flops, transcendentals=0, bytes_accessed=1 << 20),
         compiler_params=pltpu.CompilerParams(vmem_limit_bytes=GRANT),
-    )(*scalars, *[pltpu.with_memory_space_constraint(array, pltpu.VMEM) for array in arrays])
+    )(*scalars, *arrays, *[pltpu.with_memory_space_constraint(x, pltpu.HBM) for x in outside])
+
+
+def in_memory(arrays):
+    return [pltpu.with_memory_space_constraint(array, pltpu.HBM) for array in arrays]
+
+
+def placed_on_chip(arrays):
+    return [pltpu.with_memory_space_constraint(array, pltpu.VMEM) for array in arrays]
 
 
 def body(
@@ -245,7 +280,7 @@
     device = lax.axis_index(ALL).reshape(1)
     owners = block_order // per_device
     slots = block_order % per_device
-    weights_of = [inducing_weights] + [
+    others = [
         lax.ppermute(inducing_weights, "cols", [(i, i ^ mask) for i in range(col_count)])
         for mask in range(1, col_count)
     ]
@@ -254,63 +289,76 @@
     tile_flops = 2 * LANES * points_dev
     half = (targets.shape[0] // 2, points_dev)
     halves = [on_chip(half, jnp.bfloat16)] * 2
-    out, scaled = call(
+    out, scaled, table = call(
         functools.partial(pick_kernel, per_anchor),
         [
             on_chip((count, per_anchor + per_block, UNIT, LANES), jnp.float32),
             on_chip(points.shape, jnp.float32),
+            on_chip((1 + 2 * step_count, 8, LANES), jnp.int32),
         ],
-        [device],
-        [inducing_index[None, :], points, lengthscales[None, :]],
+        in_memory([device, owners, slots]),
+        in_memory([inducing_index[None, :], points, lengthscales[None, :]]),
         [],
         2 * 3 * dims * points_dev * anchor_count,
     )
     got = lax.all_to_all(out, ALL, 0, 0)
-    (spread,) = call(
-        functools.partial(merge_kernel, per_anchor),
-        [on_chip((count, per_anchor + step_count * per_block, UNIT, LANES), jnp.float32)],
-        [owners],
-        [got],
+    (copies,) = call(
+        functools.partial(merge_kernel, per_anchor, step_count),
+        [
+            on_chip((count, per_anchor + step_count * per_block, UNIT, LANES), jnp.float32),
+        ],
+        [],
+        placed_on_chip([table, got]),
         [],
         1 << 20,
-    )
-    got = lax.all_to_all(spread, ALL, 0, 0)
+        others,
+    )
+    shared = lax.all_to_all(copies, ALL, 0, 0)
     residual, mine, other = call(
-        functools.partial(warm_kernel, per_anchor),
+        functools.partial(warm_kernel, per_anchor, step_count),
         [on_chip(targets.shape, jnp.float32), *halves],
-        [device, slots],
-        [got, scaled, *weights_of, targets, block_inverse],
+        [],
+        placed_on_chip([table, shared, scaled, block_inverse]),
         [
             pltpu.VMEM((dims, anchor_count), jnp.float32),
             pltpu.VMEM((anchor_count, LANES), jnp.bfloat16),
             pltpu.VMEM(targets.shape, jnp.bfloat16),
+            pltpu.VMEM((col_count, *inducing_weights.shape), jnp.bfloat16),
+            pltpu.VMEM(targets.shape, jnp.float32),
+            pltpu.SemaphoreType.DMA((col_count + 1,)),
         ],
         tile_flops * anchor_count,
-    )
-    weights = jnp.zeros_like(residual)
+        [inducing_weights, *others, targets],
+    )
+    weights = None
     for step_no in range(step_count):
         last = step_no == step_count - 1
-        held, partner = spread_step(mine, other, step_no, device, owners)
+        held, partner = spread_step(mine, other, step_no, table)
         (tile,) = call(
             functools.partial(tile_kernel, per_anchor + step_no * per_block, per_block),
             [on_chip((points_dev, points_dev), jnp.bfloat16)],
             [],
-            [got, scaled],
+            placed_on_chip([shared, scaled]),
             [pltpu.VMEM(points.shape, jnp.float32), pltpu.VMEM((points_dev, LANES), jnp.bfloat16)],
             tile_flops * points_dev,
         )
-        state = [held, partner, tile, residual, weights]
+        state = [table, held, partner, tile, residual]
+        if step_no:
+            state.append(weights)
+        if not last:
+            state.append(block_inverse)
         shape = jax.ShapeDtypeStruct if last else on_chip
         results = call(
-            functools.partial(update_kernel, step_no, last),
+            functools.partial(update_kernel, step_no, step_count),
             [shape(targets.shape, jnp.float32)] * 2 + ([] if last else halves),
-            [device, owners, slots],
-            state if last else state + [block_inverse],
+            [],
+            placed_on_chip(state),
             [pltpu.VMEM(targets.shape, jnp.bfloat16)],
             tile_flops * points_dev // 4,
         )
-        residual, weights = results[:2]
-        mine, other = results[2:] if not last else (None, None)
+        residual, weights, *rest = results
+        if not last:
+            mine, other = rest
     return (residual, weights)
 
 

time: 107 us -> 98.6 us (0.921)
  Pallas kernels: 17.7 us -> 12.2 us
  starting transfers between devices: 29.3 us -> 34 us
  local copies, waits for them, and re-layouts: 4.8 us -> 0.59 us
  waiting for transfers between devices: 37.9 us -> 34.8 us
    pallas_call x18, Pallas kernels: 17.7 us -> 12.2 us  [call(): pl.pallas_call(kernel, out_shape=out_shape, in_specs=[pl.BlockSpec(memory...]
    unnamed x16 -> x8, local copies, waits for them, and re-layouts: 4.78 us -> 0.02 us
    all_to_all x1, starting transfers between devices: 2.62 us -> 7.32 us  [body(): got = lax.all_to_all(out, ALL, 0, 0)]
    all_to_all x1, waiting for transfers between devices: 3.84 us -> 1.51 us  [body(): got = lax.all_to_all(out, ALL, 0, 0)]
where the time goes in v1:
time: 98.6 us; the launch traced here: 98.4 us
  waiting for transfers between devices  34.8 us (35%)
  starting transfers between devices  34 us (34%)
  blocking collectives  15.9 us (16%)
  Pallas kernels  12.2 us (12%)
    ppermute x24, waiting for transfers between devices, exchange(): return lax.ppermute(value, ALL, [(i, i ^ mask) for i in range(count)])  27.8 us
    ppermute x24, starting transfers between devices, exchange(): return lax.ppermute(value, ALL, [(i, i ^ mask) for i in range(count)])  24.7 us
    all_to_all x1, blocking collectives, body(): shared = lax.all_to_all(copies, ALL, 0, 0)  15.9 us
    pallas_call x18, Pallas kernels, call(): pl.pallas_call(kernel, out_shape=out_shape, in_specs=[pl.BlockSpec(memory...  12.2 us
    all_to_all x1, starting transfers between devices, body(): got = lax.all_to_all(out, ALL, 0, 0)  7.32 us
    ppermute x3, waiting for transfers between devices, body(): lax.ppermute(inducing_weights, 'cols', [(i, i ^ mask) for i in range(col_...  5.47 us
  transfers between devices with their start and end apart: 28, of which 25 were waited for; matrix products, arithmetic and copies ran while one was open for 0% of the time, Pallas kernels for 2%

profile of v1, /device:TPU:0, one launch (start us, length us, event | category | flops | bytes accessed | tf_op | source)
XLA Modules:
  0.0 98.4 jit_solution(16137855453890213390)
XLA Ops:
  0.6 0.6 ne.14.slots_ref
  1.2 2.5 %shard_map.86 = (f32[32,3,4,128]{3,2,1,0:T(4,128)}, f32[16,1024]{1,0:T(8,128)S(1)}, s32[7,8,128]{2,1,0:T(8,128)S(1)}) custom-call(s32[1]{0:T(128)} %bitcast.device_ref, s32[3]{0:T(128)} %owners_ref, s32[3]{0:T(128)} %ne.14.slots_ref, s32[1,2048]{1,0:T(1,128)} %bitcast.3, f32[16,1024]{1,0:T(8,128)} %points_ref.1, f32[1,16]{1,0:T(1,128)} %bitcast.4), custom_call_target="tpu_custom_call" | custom-call | flops 201326592 | bytes 1048576 | tf_op jit(solution)/shard_map/pallas_call | solution.py:253
  3.7 7.3 %all-to-all-start = ((f32[32,3,4,128]{3,2,1,0:T(4,128)}), f32[32,3,4,128]{3,2,1,0:T(4,128)S(1)}, u32[]{:S(2)}, u32[]{:S(2)}) async-start(f32[32,3,4,128]{3,2,1,0:T(4,128)} %get-tuple-element.17), calls=%async_computation | async-start | bytes 393216 | tf_op jit(solution)/shard_map/all_to_all | solution.py:304
  11.1 0.3 collective-permute-start
  11.4 1.6 %collective-permute-start.1 = (bf16[64,512]{1,0:T(8,128)(2,1)}, bf16[64,512]{1,0:T(8,128)(2,1)S(1)}, u32[]{:S(2)}, u32[]{:S(2)}) collective-permute-start(bf16[64,512]{1,0:T(8,128)(2,1)} %refs_0_.1), channel_id=1, source_target_pairs={{0,2},{1,3},{2,0},{3,1},{4,6},{5,7},{6,4},{7,5},{8,10},{9,11},{10,... | collective-permute-start | bytes 196616 | tf_op jit(solution)/shard_map/ppermute | solution.py:284
  13.0 4.6 %collective-permute-done.1.refs_1_.refs_2_ = bf16[64,512]{1,0:T(8,128)(2,1)S(1)} collective-permute-done((bf16[64,512]{1,0:T(8,128)(2,1)}, bf16[64,512]{1,0:T(8,128)(2,1)S(1)}, u32[]{:S(2)}, u32[]{:S(2)}) %collective-permute-start.1) | collective-permute-done | bytes 65568 | tf_op jit(solution)/shard_map/ppermute | solution.py:284
  17.6 0.9 collective-permute-done.2.refs_2_.refs_3_
  18.5 1.5 %all-to-all-done.got_ref = f32[32,3,4,128]{3,2,1,0:T(4,128)S(1)} async-done(((f32[32,3,4,128]{3,2,1,0:T(4,128)}), f32[32,3,4,128]{3,2,1,0:T(4,128)S(1)}, u32[]{:S(2)}, u32[]{:S(2)}) %all-to-all-start) | async-done | bytes 196640 | tf_op jit(solution)/shard_map/all_to_all | solution.py:304
  20.0 0.1 shard_map.87
  20.1 15.9 %all_to_all.10.got_ref = f32[32,5,4,128]{3,2,1,0:T(4,128)S(1)} all-to-all(f32[32,5,4,128]{3,2,1,0:T(4,128)S(1)} %shard_map.87), channel_id=1, replica_groups=mesh['rows'=8,'cols'=4] {'rows','cols'}, dimensions={0} | all-to-all | bytes 655360 | tf_op jit(solution)/shard_map/all_to_all | solution.py:316
  36.0 3.8 %shard_map.88 = (f32[64,1024]{1,0:T(8,128)S(1)}, bf16[32,1024]{1,0:T(8,128)(2,1)S(1)}, bf16[32,1024]{1,0:T(8,128)(2,1)S(1)}) custom-call(s32[7,8,128]{2,1,0:T(8,128)S(1)} %get-tuple-element.16.table_ref, f32[32,5,4,128]{3,2,1,0:T(4,128)S(1)} %all_to_all.10.got_ref, f32[16,1024]{1,0:T(8,128)S(1)} %get-tuple-element.18.scaled_ref, ...), custom_call_target="tpu_custom_call" | custom-call | flops 536870912 | bytes 1048576 | tf_op jit(solution)/shard_map/pallas_call | solution.py:253
  39.9 0.1 collective-permute-start.3
  39.9 1.2 %collective-permute-done.3.refs_1_ = bf16[32,1024]{1,0:T(8,128)(2,1)S(1)} collective-permute-done((bf16[32,1024]{1,0:T(8,128)(2,1)S(1)}, bf16[32,1024]{1,0:T(8,128)(2,1)S(1)}, u32[]{:S(2)}, u32[]{:S(2)}) %collective-permute-start.3) | collective-permute-done | bytes 65568 | tf_op jit(solution)/shard_map/ppermute | solution.py:25
  41.2 0.4 collective-permute-start.4
  41.7 1.3 %collective-permute-start.5 = (bf16[32,1024]{1,0:T(8,128)(2,1)S(1)}, bf16[32,1024]{1,0:T(8,128)(2,1)S(1)}, u32[]{:S(2)}, u32[]{:S(2)}) collective-permute-start(bf16[32,1024]{1,0:T(8,128)(2,1)S(1)} %shard_map.89.refs_0_), channel_id=1, source_target_pairs={{0,4},{1,5},{2,6},{3,7},{4,0},{5,1},{6,2},{7,3},{8,12},{9,13},{10,... | collective-permute-start | bytes 196616 | tf_op jit(solution)/shard_map/ppermute | solution.py:25
  43.0 1.8 %collective-permute-start.6 = (bf16[32,1024]{1,0:T(8,128)(2,1)S(1)}, bf16[32,1024]{1,0:T(8,128)(2,1)S(1)}, u32[]{:S(2)}, u32[]{:S(2)}) collective-permute-start(bf16[32,1024]{1,0:T(8,128)(2,1)S(1)} %shard_map.89.refs_0_), channel_id=1, source_target_pairs={{0,6},{1,7},{2,4},{3,5},{4,2},{5,3},{6,0},{7,1},{8,14},{9,15},{10,... | collective-permute-start | bytes 196616 | tf_op jit(solution)/shard_map/ppermute | solution.py:25
  44.8 0.8 collective-permute-done.4.refs_1_
  45.6 0.6 collective-permute-done.5.refs_2_
  46.1 2.0 %collective-permute-done.6.refs_3_ = bf16[32,1024]{1,0:T(8,128)(2,1)S(1)} collective-permute-done((bf16[32,1024]{1,0:T(8,128)(2,1)S(1)}, bf16[32,1024]{1,0:T(8,128)(2,1)S(1)}, u32[]{:S(2)}, u32[]{:S(2)}) %collective-permute-start.6) | collective-permute-done | bytes 65568 | tf_op jit(solution)/shard_map/ppermute | solution.py:25
  48.2 0.1 shard_map.90.refs_0_
  48.2 0.7 collective-permute-start.7
  49.0 1.3 %collective-permute-start.8 = (bf16[32,1024]{1,0:T(8,128)(2,1)S(1)}, bf16[32,1024]{1,0:T(8,128)(2,1)S(1)}, u32[]{:S(2)}, u32[]{:S(2)}) collective-permute-start(bf16[32,1024]{1,0:T(8,128)(2,1)S(1)} %shard_map.90.refs_0_), channel_id=1, source_target_pairs={{0,16},{1,17},{2,18},{3,19},{4,20},{5,21},{6,22},{7,23},{8,24},{9,... | collective-permute-start | bytes 196616 | tf_op jit(solution)/shard_map/ppermute | solution.py:25
  50.3 2.4 %collective-permute-start.9 = (bf16[32,1024]{1,0:T(8,128)(2,1)S(1)}, bf16[32,1024]{1,0:T(8,128)(2,1)S(1)}, u32[]{:S(2)}, u32[]{:S(2)}) collective-permute-start(bf16[32,1024]{1,0:T(8,128)(2,1)S(1)} %shard_map.90.refs_0_), channel_id=1, source_target_pairs={{0,24},{1,25},{2,26},{3,27},{4,28},{5,29},{6,30},{7,31},{8,16},{9,... | collective-permute-start | bytes 196616 | tf_op jit(solution)/shard_map/ppermute | solution.py:25
  52.7 2.6 %collective-permute-done.8.refs_2_ = bf16[32,1024]{1,0:T(8,128)(2,1)S(1)} collective-permute-done((bf16[32,1024]{1,0:T(8,128)(2,1)S(1)}, bf16[32,1024]{1,0:T(8,128)(2,1)S(1)}, u32[]{:S(2)}, u32[]{:S(2)}) %collective-permute-start.8) | collective-permute-done | bytes 65568 | tf_op jit(solution)/shard_map/ppermute | solution.py:25
  55.3 1.1 %collective-permute-done.9.refs_3_ = bf16[32,1024]{1,0:T(8,128)(2,1)S(1)} collective-permute-done((bf16[32,1024]{1,0:T(8,128)(2,1)S(1)}, bf16[32,1024]{1,0:T(8,128)(2,1)S(1)}, u32[]{:S(2)}, u32[]{:S(2)}) %collective-permute-start.9) | collective-permute-done | bytes 65568 | tf_op jit(solution)/shard_map/ppermute | solution.py:25
  56.5 0.1 collective-permute-start.10
  56.6 0.8 shard_map.92.tile_ref
  57.3 0.5 collective-permute-done.10.partner_ref
  57.8 0.9 shard_map.93
  58.7 0.2 collective-permute-start.11
  58.9 1.1 %collective-permute-done.11.refs_1_ = bf16[32,1024]{1,0:T(8,128)(2,1)S(1)} collective-permute-done((bf16[32,1024]{1,0:T(8,128)(2,1)S(1)}, bf16[32,1024]{1,0:T(8,128)(2,1)S(1)}, u32[]{:S(2)}, u32[]{:S(2)}) %collective-permute-start.11) | collective-permute-done | bytes 65568 | tf_op jit(solution)/shard_map/ppermute | solution.py:25
  60.1 0.8 collective-permute-start.12
  60.8 1.2 %collective-permute-start.13 = (bf16[32,1024]{1,0:T(8,128)(2,1)S(1)}, bf16[32,1024]{1,0:T(8,128)(2,1)S(1)}, u32[]{:S(2)}, u32[]{:S(2)}) collective-permute-start(bf16[32,1024]{1,0:T(8,128)(2,1)S(1)} %shard_map.94.refs_0_), channel_id=1, source_target_pairs={{0,4},{1,5},{2,6},{3,7},{4,0},{5,1},{6,2},{7,3},{8,12},{9,13},{10,... | collective-permute-start | bytes 196616 | tf_op jit(solution)/shard_map/ppermute | solution.py:25
  62.1 1.5 %collective-permute-start.14 = (bf16[32,1024]{1,0:T(8,128)(2,1)S(1)}, bf16[32,1024]{1,0:T(8,128)(2,1)S(1)}, u32[]{:S(2)}, u32[]{:S(2)}) collective-permute-start(bf16[32,1024]{1,0:T(8,128)(2,1)S(1)} %shard_map.94.refs_0_), channel_id=1, source_target_pairs={{0,6},{1,7},{2,4},{3,5},{4,2},{5,3},{6,0},{7,1},{8,14},{9,15},{10,... | collective-permute-start | bytes 196616 | tf_op jit(solution)/shard_map/ppermute | solution.py:25
  63.6 0.8 collective-permute-done.12.refs_1_
  64.4 1.3 %collective-permute-done.13.refs_2_ = bf16[32,1024]{1,0:T(8,128)(2,1)S(1)} collective-permute-done((bf16[32,1024]{1,0:T(8,128)(2,1)S(1)}, bf16[32,1024]{1,0:T(8,128)(2,1)S(1)}, u32[]{:S(2)}, u32[]{:S(2)}) %collective-permute-start.13) | collective-permute-done | bytes 65568 | tf_op jit(solution)/shard_map/ppermute | solution.py:25
  65.7 1.6 %collective-permute-done.14.refs_3_ = bf16[32,1024]{1,0:T(8,128)(2,1)S(1)} collective-permute-done((bf16[32,1024]{1,0:T(8,128)(2,1)S(1)}, bf16[32,1024]{1,0:T(8,128)(2,1)S(1)}, u32[]{:S(2)}, u32[]{:S(2)}) %collective-permute-start.14) | collective-permute-done | bytes 65568 | tf_op jit(solution)/shard_map/ppermute | solution.py:25
  67.3 1.2 %collective-permute-start.15 = (bf16[32,1024]{1,0:T(8,128)(2,1)S(1)}, bf16[32,1024]{1,0:T(8,128)(2,1)S(1)}, u32[]{:S(2)}, u32[]{:S(2)}) collective-permute-start(bf16[32,1024]{1,0:T(8,128)(2,1)S(1)} %shard_map.95.refs_0_), channel_id=1, source_target_pairs={{0,8},{1,9},{2,10},{3,11},{4,12},{5,13},{6,14},{7,15},{8,0},{9,1},... | collective-permute-start | bytes 196616 | tf_op jit(solution)/shard_map/ppermute | solution.py:25
  68.5 2.2 %collective-permute-start.16 = (bf16[32,1024]{1,0:T(8,128)(2,1)S(1)}, bf16[32,1024]{1,0:T(8,128)(2,1)S(1)}, u32[]{:S(2)}, u32[]{:S(2)}) collective-permute-start(bf16[32,1024]{1,0:T(8,128)(2,1)S(1)} %shard_map.95.refs_0_), channel_id=1, source_target_pairs={{0,16},{1,17},{2,18},{3,19},{4,20},{5,21},{6,22},{7,23},{8,24},{9,... | collective-permute-start | bytes 196616 | tf_op jit(solution)/shard_map/ppermute | solution.py:25
  70.7 1.1 %collective-permute-start.17 = (bf16[32,1024]{1,0:T(8,128)(2,1)S(1)}, bf16[32,1024]{1,0:T(8,128)(2,1)S(1)}, u32[]{:S(2)}, u32[]{:S(2)}) collective-permute-start(bf16[32,1024]{1,0:T(8,128)(2,1)S(1)} %shard_map.95.refs_0_), channel_id=1, source_target_pairs={{0,24},{1,25},{2,26},{3,27},{4,28},{5,29},{6,30},{7,31},{8,16},{9,... | collective-permute-start | bytes 196616 | tf_op jit(solution)/shard_map/ppermute | solution.py:25
  71.8 0.2 collective-permute-done.15.refs_1_
  72.0 3.1 %collective-permute-done.16.refs_2_ = bf16[32,1024]{1,0:T(8,128)(2,1)S(1)} collective-permute-done((bf16[32,1024]{1,0:T(8,128)(2,1)S(1)}, bf16[32,1024]{1,0:T(8,128)(2,1)S(1)}, u32[]{:S(2)}, u32[]{:S(2)}) %collective-permute-start.16) | collective-permute-done | bytes 65568 | tf_op jit(solution)/shard_map/ppermute | solution.py:25
  75.1 1.6 %collective-permute-done.17.refs_3_ = bf16[32,1024]{1,0:T(8,128)(2,1)S(1)} collective-permute-done((bf16[32,1024]{1,0:T(8,128)(2,1)S(1)}, bf16[32,1024]{1,0:T(8,128)(2,1)S(1)}, u32[]{:S(2)}, u32[]{:S(2)}) %collective-permute-start.17) | collective-permute-done | bytes 65568 | tf_op jit(solution)/shard_map/ppermute | solution.py:25
  76.8 0.1 collective-permute-start.18
  76.9 0.8 shard_map.97.tile_ref
  77.7 0.5 collective-permute-done.18.partner_ref
  78.1 0.9 shard_map.98
  79.0 0.2 collective-permute-start.19
  79.2 1.1 %collective-permute-done.19.refs_1_ = bf16[32,1024]{1,0:T(8,128)(2,1)S(1)} collective-permute-done((bf16[32,1024]{1,0:T(8,128)(2,1)S(1)}, bf16[32,1024]{1,0:T(8,128)(2,1)S(1)}, u32[]{:S(2)}, u32[]{:S(2)}) %collective-permute-start.19) | collective-permute-done | bytes 65568 | tf_op jit(solution)/shard_map/ppermute | solution.py:25
  80.4 0.7 collective-permute-start.20
  81.1 1.1 %collective-permute-start.21 = (bf16[32,1024]{1,0:T(8,128)(2,1)S(1)}, bf16[32,1024]{1,0:T(8,128)(2,1)S(1)}, u32[]{:S(2)}, u32[]{:S(2)}) collective-permute-start(bf16[32,1024]{1,0:T(8,128)(2,1)S(1)} %shard_map.99.refs_0_), channel_id=1, source_target_pairs={{0,4},{1,5},{2,6},{3,7},{4,0},{5,1},{6,2},{7,3},{8,12},{9,13},{10,... | collective-permute-start | bytes 196616 | tf_op jit(solution)/shard_map/ppermute | solution.py:25
  82.2 1.8 %collective-permute-start.22 = (bf16[32,1024]{1,0:T(8,128)(2,1)S(1)}, bf16[32,1024]{1,0:T(8,128)(2,1)S(1)}, u32[]{:S(2)}, u32[]{:S(2)}) collective-permute-start(bf16[32,1024]{1,0:T(8,128)(2,1)S(1)} %shard_map.99.refs_0_), channel_id=1, source_target_pairs={{0,6},{1,7},{2,4},{3,5},{4,2},{5,3},{6,0},{7,1},{8,14},{9,15},{10,... | collective-permute-start | bytes 196616 | tf_op jit(solution)/shard_map/ppermute | solution.py:25
  83.9 0.8 collective-permute-done.20.refs_1_
  84.7 1.1 %collective-permute-done.21.refs_2_ = bf16[32,1024]{1,0:T(8,128)(2,1)S(1)} collective-permute-done((bf16[32,1024]{1,0:T(8,128)(2,1)S(1)}, bf16[32,1024]{1,0:T(8,128)(2,1)S(1)}, u32[]{:S(2)}, u32[]{:S(2)}) %collective-permute-start.21) | collective-permute-done | bytes 65568 | tf_op jit(solution)/shard_map/ppermute | solution.py:25
  85.8 1.6 %collective-permute-done.22.refs_3_ = bf16[32,1024]{1,0:T(8,128)(2,1)S(1)} collective-permute-done((bf16[32,1024]{1,0:T(8,128)(2,1)S(1)}, bf16[32,1024]{1,0:T(8,128)(2,1)S(1)}, u32[]{:S(2)}, u32[]{:S(2)}) %collective-permute-start.22) | collective-permute-done | bytes 65568 | tf_op jit(solution)/shard_map/ppermute | solution.py:25
  87.5 0.1 collective-permute-start.23
  87.5 2.1 %collective-permute-start.24 = (bf16[32,1024]{1,0:T(8,128)(2,1)S(1)}, bf16[32,1024]{1,0:T(8,128)(2,1)S(1)}, u32[]{:S(2)}, u32[]{:S(2)}) collective-permute-start(bf16[32,1024]{1,0:T(8,128)(2,1)S(1)} %shard_map.100.refs_0_), channel_id=1, source_target_pairs={{0,16},{1,17},{2,18},{3,19},{4,20},{5,21},{6,22},{7,23},{8,24},{9,... | collective-permute-start | bytes 196616 | tf_op jit(solution)/shard_map/ppermute | solution.py:25
  89.6 2.3 %collective-permute-start.25 = (bf16[32,1024]{1,0:T(8,128)(2,1)S(1)}, bf16[32,1024]{1,0:T(8,128)(2,1)S(1)}, u32[]{:S(2)}, u32[]{:S(2)}) collective-permute-start(bf16[32,1024]{1,0:T(8,128)(2,1)S(1)} %shard_map.100.refs_0_), channel_id=1, source_target_pairs={{0,24},{1,25},{2,26},{3,27},{4,28},{5,29},{6,30},{7,31},{8,16},{9,... | collective-permute-start | bytes 196616 | tf_op jit(solution)/shard_map/ppermute | solution.py:25
  91.9 2.4 %collective-permute-done.24.refs_2_ = bf16[32,1024]{1,0:T(8,128)(2,1)S(1)} collective-permute-done((bf16[32,1024]{1,0:T(8,128)(2,1)S(1)}, bf16[32,1024]{1,0:T(8,128)(2,1)S(1)}, u32[]{:S(2)}, u32[]{:S(2)}) %collective-permute-start.24) | collective-permute-done | bytes 65568 | tf_op jit(solution)/shard_map/ppermute | solution.py:25
  94.4 1.4 %collective-permute-done.25.refs_3_ = bf16[32,1024]{1,0:T(8,128)(2,1)S(1)} collective-permute-done((bf16[32,1024]{1,0:T(8,128)(2,1)S(1)}, bf16[32,1024]{1,0:T(8,128)(2,1)S(1)}, u32[]{:S(2)}, u32[]{:S(2)}) %collective-permute-start.25) | collective-permute-done | bytes 65568 | tf_op jit(solution)/shard_map/ppermute | solution.py:25
  95.8 0.1 collective-permute-start.26
  95.9 0.8 shard_map.102.tile_ref
  96.7 0.5 collective-permute-done.26.partner_ref
  97.1 1.2 %shard_map.103 = (f32[64,1024]{1,0:T(8,128)}, f32[64,1024]{1,0:T(8,128)}) custom-call(s32[7,8,128]{2,1,0:T(8,128)S(1)} %get-tuple-element.16.table_ref, bf16[32,1024]{1,0:T(8,128)(2,1)S(1)} %shard_map.101.held_ref, bf16[32,1024]{1,0:T(8,128)(2,1)S(1)} %collective-permute-done.26.partner_ref, bf16[1024,1024]{1,0:T(8,128)(2,1)S(1)} %shard_map.102.tile_ref, ...), custom_call_target="tpu_custom_call" | custom-call | flops 67108864 | bytes 1048576 | tf_op jit(solution)/shard_map/pallas_call | solution.py:253
  (20 shorter events, 0.4 us)
Async XLA Ops:
  0.6 35.4 %copy-start = (bf16[1,1024,1024]{2,1,0:T(8,128)(2,1)S(1)}, bf16[1,1024,1024]{2,1,0:T(8,128)(2,1)}, u32[]{:S(2)}) copy-start(bf16[1,1024,1024]{2,1,0:T(8,128)(2,1)} %refs_2_.1) | copy-start | bytes 6291460
  3.7 16.3 %all-to-all-start = ((f32[32,3,4,128]{3,2,1,0:T(4,128)}), f32[32,3,4,128]{3,2,1,0:T(4,128)S(1)}, u32[]{:S(2)}, u32[]{:S(2)}) async-start(f32[32,3,4,128]{3,2,1,0:T(4,128)} %get-tuple-element.17), calls=%async_computation | async-start | bytes 393216 | tf_op jit(solution)/shard_map/all_to_all | solution.py:304
  11.1 2.0 %collective-permute-start = (bf16[64,512]{1,0:T(8,128)(2,1)}, bf16[64,512]{1,0:T(8,128)(2,1)S(1)}, u32[]{:S(2)}, u32[]{:S(2)}) collective-permute-start(bf16[64,512]{1,0:T(8,128)(2,1)} %refs_0_.1), channel_id=1, source_target_pairs={{0,1},{1,0},{2,3},{3,2},{4,5},{5,4},{6,7},{7,6},{8,9},{9,8},{10,11... | collective-permute-start | bytes 196616 | tf_op jit(solution)/shard_map/ppermute | solution.py:284
  11.4 6.2 %collective-permute-start.1 = (bf16[64,512]{1,0:T(8,128)(2,1)}, bf16[64,512]{1,0:T(8,128)(2,1)S(1)}, u32[]{:S(2)}, u32[]{:S(2)}) collective-permute-start(bf16[64,512]{1,0:T(8,128)(2,1)} %refs_0_.1), channel_id=1, source_target_pairs={{0,2},{1,3},{2,0},{3,1},{4,6},{5,7},{6,4},{7,5},{8,10},{9,11},{10,... | collective-permute-start | bytes 196616 | tf_op jit(solution)/shard_map/ppermute | solution.py:284
  13.0 5.5 %collective-permute-start.2 = (bf16[64,512]{1,0:T(8,128)(2,1)}, bf16[64,512]{1,0:T(8,128)(2,1)S(1)}, u32[]{:S(2)}, u32[]{:S(2)}) collective-permute-start(bf16[64,512]{1,0:T(8,128)(2,1)} %refs_0_.1), channel_id=1, source_target_pairs={{0,3},{1,2},{2,1},{3,0},{4,7},{5,6},{6,5},{7,4},{8,11},{9,10},{10,... | collective-permute-start | bytes 196616 | tf_op jit(solution)/shard_map/ppermute | solution.py:284
  13.0 7.0 %copy-start.1 = (bf16[64,512]{1,0:T(8,128)(2,1)}, bf16[64,512]{1,0:T(8,128)(2,1)S(1)}, u32[]{:S(2)}) copy-start(bf16[64,512]{1,0:T(8,128)(2,1)S(1)} %collective-permute-done.refs_0_.refs_1_) | copy-start | bytes 196612
  17.6 2.4 %copy-start.2 = (bf16[64,512]{1,0:T(8,128)(2,1)}, bf16[64,512]{1,0:T(8,128)(2,1)S(1)}, u32[]{:S(2)}) copy-start(bf16[64,512]{1,0:T(8,128)(2,1)S(1)} %collective-permute-done.1.refs_1_.refs_2_) | copy-start | bytes 196612
  18.5 1.5 %copy-start.3 = (bf16[64,512]{1,0:T(8,128)(2,1)}, bf16[64,512]{1,0:T(8,128)(2,1)S(1)}, u32[]{:S(2)}) copy-start(bf16[64,512]{1,0:T(8,128)(2,1)S(1)} %collective-permute-done.2.refs_2_.refs_3_) | copy-start | bytes 196612
  39.9 1.3 %collective-permute-start.3 = (bf16[32,1024]{1,0:T(8,128)(2,1)S(1)}, bf16[32,1024]{1,0:T(8,128)(2,1)S(1)}, u32[]{:S(2)}, u32[]{:S(2)}) collective-permute-start(bf16[32,1024]{1,0:T(8,128)(2,1)S(1)} %get-tuple-element.20), channel_id=1, source_target_pairs={{0,1},{1,0},{2,3},{3,2},{4,5},{5,4},{6,7},{7,6},{8,9},{9,8},{10,11... | collective-permute-start | bytes 196616 | tf_op jit(solution)/shard_map/ppermute | solution.py:25
  41.2 4.3 %collective-permute-start.4 = (bf16[32,1024]{1,0:T(8,128)(2,1)S(1)}, bf16[32,1024]{1,0:T(8,128)(2,1)S(1)}, u32[]{:S(2)}, u32[]{:S(2)}) collective-permute-start(bf16[32,1024]{1,0:T(8,128)(2,1)S(1)} %shard_map.89.refs_0_), channel_id=1, source_target_pairs={{0,2},{1,3},{2,0},{3,1},{4,6},{5,7},{6,4},{7,5},{8,10},{9,11},{10,... | collective-permute-start | bytes 196616 | tf_op jit(solution)/shard_map/ppermute | solution.py:25
  41.7 4.5 %collective-permute-start.5 = (bf16[32,1024]{1,0:T(8,128)(2,1)S(1)}, bf16[32,1024]{1,0:T(8,128)(2,1)S(1)}, u32[]{:S(2)}, u32[]{:S(2)}) collective-permute-start(bf16[32,1024]{1,0:T(8,128)(2,1)S(1)} %shard_map.89.refs_0_), channel_id=1, source_target_pairs={{0,4},{1,5},{2,6},{3,7},{4,0},{5,1},{6,2},{7,3},{8,12},{9,13},{10,... | collective-permute-start | bytes 196616 | tf_op jit(solution)/shard_map/ppermute | solution.py:25
  43.0 5.2 %collective-permute-start.6 = (bf16[32,1024]{1,0:T(8,128)(2,1)S(1)}, bf16[32,1024]{1,0:T(8,128)(2,1)S(1)}, u32[]{:S(2)}, u32[]{:S(2)}) collective-permute-start(bf16[32,1024]{1,0:T(8,128)(2,1)S(1)} %shard_map.89.refs_0_), channel_id=1, source_target_pairs={{0,6},{1,7},{2,4},{3,5},{4,2},{5,3},{6,0},{7,1},{8,14},{9,15},{10,... | collective-permute-start | bytes 196616 | tf_op jit(solution)/shard_map/ppermute | solution.py:25
  48.2 4.5 %collective-permute-start.7 = (bf16[32,1024]{1,0:T(8,128)(2,1)S(1)}, bf16[32,1024]{1,0:T(8,128)(2,1)S(1)}, u32[]{:S(2)}, u32[]{:S(2)}) collective-permute-start(bf16[32,1024]{1,0:T(8,128)(2,1)S(1)} %shard_map.90.refs_0_), channel_id=1, source_target_pairs={{0,8},{1,9},{2,10},{3,11},{4,12},{5,13},{6,14},{7,15},{8,0},{9,1},... | collective-permute-start | bytes 196616 | tf_op jit(solution)/shard_map/ppermute | solution.py:25
  49.0 6.4 %collective-permute-start.8 = (bf16[32,1024]{1,0:T(8,128)(2,1)S(1)}, bf16[32,1024]{1,0:T(8,128)(2,1)S(1)}, u32[]{:S(2)}, u32[]{:S(2)}) collective-permute-start(bf16[32,1024]{1,0:T(8,128)(2,1)S(1)} %shard_map.90.refs_0_), channel_id=1, source_target_pairs={{0,16},{1,17},{2,18},{3,19},{4,20},{5,21},{6,22},{7,23},{8,24},{9,... | collective-permute-start | bytes 196616 | tf_op jit(solution)/shard_map/ppermute | solution.py:25
  50.3 6.2 %collective-permute-start.9 = (bf16[32,1024]{1,0:T(8,128)(2,1)S(1)}, bf16[32,1024]{1,0:T(8,128)(2,1)S(1)}, u32[]{:S(2)}, u32[]{:S(2)}) collective-permute-start(bf16[32,1024]{1,0:T(8,128)(2,1)S(1)} %shard_map.90.refs_0_), channel_id=1, source_target_pairs={{0,24},{1,25},{2,26},{3,27},{4,28},{5,29},{6,30},{7,31},{8,16},{9,... | collective-permute-start | bytes 196616 | tf_op jit(solution)/shard_map/ppermute | solution.py:25
  56.5 1.3 %collective-permute-start.10 = (bf16[32,1024]{1,0:T(8,128)(2,1)S(1)}, bf16[32,1024]{1,0:T(8,128)(2,1)S(1)}, u32[]{:S(2)}, u32[]{:S(2)}) collective-permute-start(bf16[32,1024]{1,0:T(8,128)(2,1)S(1)} %shard_map.91.held_ref), channel_id=1, source_target_pairs={{0,1},{1,0},{2,3},{3,2},{4,5},{5,4},{6,7},{7,6},{8,9},{9,8},{10,11... | collective-permute-start | bytes 196616 | tf_op jit(solution)/shard_map/ppermute | solution.py:25
  58.7 1.3 %collective-permute-start.11 = (bf16[32,1024]{1,0:T(8,128)(2,1)S(1)}, bf16[32,1024]{1,0:T(8,128)(2,1)S(1)}, u32[]{:S(2)}, u32[]{:S(2)}) collective-permute-start(bf16[32,1024]{1,0:T(8,128)(2,1)S(1)} %get-tuple-element.23), channel_id=1, source_target_pairs={{0,1},{1,0},{2,3},{3,2},{4,5},{5,4},{6,7},{7,6},{8,9},{9,8},{10,11... | collective-permute-start | bytes 196616 | tf_op jit(solution)/shard_map/ppermute | solution.py:25
  60.1 4.3 %collective-permute-start.12 = (bf16[32,1024]{1,0:T(8,128)(2,1)S(1)}, bf16[32,1024]{1,0:T(8,128)(2,1)S(1)}, u32[]{:S(2)}, u32[]{:S(2)}) collective-permute-start(bf16[32,1024]{1,0:T(8,128)(2,1)S(1)} %shard_map.94.refs_0_), channel_id=1, source_target_pairs={{0,2},{1,3},{2,0},{3,1},{4,6},{5,7},{6,4},{7,5},{8,10},{9,11},{10,... | collective-permute-start | bytes 196616 | tf_op jit(solution)/shard_map/ppermute | solution.py:25
  60.8 4.9 %collective-permute-start.13 = (bf16[32,1024]{1,0:T(8,128)(2,1)S(1)}, bf16[32,1024]{1,0:T(8,128)(2,1)S(1)}, u32[]{:S(2)}, u32[]{:S(2)}) collective-permute-start(bf16[32,1024]{1,0:T(8,128)(2,1)S(1)} %shard_map.94.refs_0_), channel_id=1, source_target_pairs={{0,4},{1,5},{2,6},{3,7},{4,0},{5,1},{6,2},{7,3},{8,12},{9,13},{10,... | collective-permute-start | bytes 196616 | tf_op jit(solution)/shard_map/ppermute | solution.py:25
  62.1 5.2 %collective-permute-start.14 = (bf16[32,1024]{1,0:T(8,128)(2,1)S(1)}, bf16[32,1024]{1,0:T(8,128)(2,1)S(1)}, u32[]{:S(2)}, u32[]{:S(2)}) collective-permute-start(bf16[32,1024]{1,0:T(8,128)(2,1)S(1)} %shard_map.94.refs_0_), channel_id=1, source_target_pairs={{0,6},{1,7},{2,4},{3,5},{4,2},{5,3},{6,0},{7,1},{8,14},{9,15},{10,... | collective-permute-start | bytes 196616 | tf_op jit(solution)/shard_map/ppermute | solution.py:25
  67.3 4.7 %collective-permute-start.15 = (bf16[32,1024]{1,0:T(8,128)(2,1)S(1)}, bf16[32,1024]{1,0:T(8,128)(2,1)S(1)}, u32[]{:S(2)}, u32[]{:S(2)}) collective-permute-start(bf16[32,1024]{1,0:T(8,128)(2,1)S(1)} %shard_map.95.refs_0_), channel_id=1, source_target_pairs={{0,8},{1,9},{2,10},{3,11},{4,12},{5,13},{6,14},{7,15},{8,0},{9,1},... | collective-permute-start | bytes 196616 | tf_op jit(solution)/shard_map/ppermute | solution.py:25
  68.5 6.6 %collective-permute-start.16 = (bf16[32,1024]{1,0:T(8,128)(2,1)S(1)}, bf16[32,1024]{1,0:T(8,128)(2,1)S(1)}, u32[]{:S(2)}, u32[]{:S(2)}) collective-permute-start(bf16[32,1024]{1,0:T(8,128)(2,1)S(1)} %shard_map.95.refs_0_), channel_id=1, source_target_pairs={{0,16},{1,17},{2,18},{3,19},{4,20},{5,21},{6,22},{7,23},{8,24},{9,... | collective-permute-start | bytes 196616 | tf_op jit(solution)/shard_map/ppermute | solution.py:25
  70.7 6.1 %collective-permute-start.17 = (bf16[32,1024]{1,0:T(8,128)(2,1)S(1)}, bf16[32,1024]{1,0:T(8,128)(2,1)S(1)}, u32[]{:S(2)}, u32[]{:S(2)}) collective-permute-start(bf16[32,1024]{1,0:T(8,128)(2,1)S(1)} %shard_map.95.refs_0_), channel_id=1, source_target_pairs={{0,24},{1,25},{2,26},{3,27},{4,28},{5,29},{6,30},{7,31},{8,16},{9,... | collective-permute-start | bytes 196616 | tf_op jit(solution)/shard_map/ppermute | solution.py:25
  76.8 1.3 %collective-permute-start.18 = (bf16[32,1024]{1,0:T(8,128)(2,1)S(1)}, bf16[32,1024]{1,0:T(8,128)(2,1)S(1)}, u32[]{:S(2)}, u32[]{:S(2)}) collective-permute-start(bf16[32,1024]{1,0:T(8,128)(2,1)S(1)} %shard_map.96.held_ref), channel_id=1, source_target_pairs={{0,1},{1,0},{2,3},{3,2},{4,5},{5,4},{6,7},{7,6},{8,9},{9,8},{10,11... | collective-permute-start | bytes 196616 | tf_op jit(solution)/shard_map/ppermute | solution.py:25
  79.0 1.3 %collective-permute-start.19 = (bf16[32,1024]{1,0:T(8,128)(2,1)S(1)}, bf16[32,1024]{1,0:T(8,128)(2,1)S(1)}, u32[]{:S(2)}, u32[]{:S(2)}) collective-permute-start(bf16[32,1024]{1,0:T(8,128)(2,1)S(1)} %get-tuple-element.27), channel_id=1, source_target_pairs={{0,1},{1,0},{2,3},{3,2},{4,5},{5,4},{6,7},{7,6},{8,9},{9,8},{10,11... | collective-permute-start | bytes 196616 | tf_op jit(solution)/shard_map/ppermute | solution.py:25
  80.4 4.3 %collective-permute-start.20 = (bf16[32,1024]{1,0:T(8,128)(2,1)S(1)}, bf16[32,1024]{1,0:T(8,128)(2,1)S(1)}, u32[]{:S(2)}, u32[]{:S(2)}) collective-permute-start(bf16[32,1024]{1,0:T(8,128)(2,1)S(1)} %shard_map.99.refs_0_), channel_id=1, source_target_pairs={{0,2},{1,3},{2,0},{3,1},{4,6},{5,7},{6,4},{7,5},{8,10},{9,11},{10,... | collective-permute-start | bytes 196616 | tf_op jit(solution)/shard_map/ppermute | solution.py:25
  81.1 4.7 %collective-permute-start.21 = (bf16[32,1024]{1,0:T(8,128)(2,1)S(1)}, bf16[32,1024]{1,0:T(8,128)(2,1)S(1)}, u32[]{:S(2)}, u32[]{:S(2)}) collective-permute-start(bf16[32,1024]{1,0:T(8,128)(2,1)S(1)} %shard_map.99.refs_0_), channel_id=1, source_target_pairs={{0,4},{1,5},{2,6},{3,7},{4,0},{5,1},{6,2},{7,3},{8,12},{9,13},{10,... | collective-permute-start | bytes 196616 | tf_op jit(solution)/shard_map/ppermute | solution.py:25
  82.2 5.2 %collective-permute-start.22 = (bf16[32,1024]{1,0:T(8,128)(2,1)S(1)}, bf16[32,1024]{1,0:T(8,128)(2,1)S(1)}, u32[]{:S(2)}, u32[]{:S(2)}) collective-permute-start(bf16[32,1024]{1,0:T(8,128)(2,1)S(1)} %shard_map.99.refs_0_), channel_id=1, source_target_pairs={{0,6},{1,7},{2,4},{3,5},{4,2},{5,3},{6,0},{7,1},{8,14},{9,15},{10,... | collective-permute-start | bytes 196616 | tf_op jit(solution)/shard_map/ppermute | solution.py:25
  87.5 4.5 %collective-permute-start.23 = (bf16[32,1024]{1,0:T(8,128)(2,1)S(1)}, bf16[32,1024]{1,0:T(8,128)(2,1)S(1)}, u32[]{:S(2)}, u32[]{:S(2)}) collective-permute-start(bf16[32,1024]{1,0:T(8,128)(2,1)S(1)} %shard_map.100.refs_0_), channel_id=1, source_target_pairs={{0,8},{1,9},{2,10},{3,11},{4,12},{5,13},{6,14},{7,15},{8,0},{9,1},... | collective-permute-start | bytes 196616 | tf_op jit(solution)/shard_map/ppermute | solution.py:25
  87.5 6.8 %collective-permute-start.24 = (bf16[32,1024]{1,0:T(8,128)(2,1)S(1)}, bf16[32,1024]{1,0:T(8,128)(2,1)S(1)}, u32[]{:S(2)}, u32[]{:S(2)}) collective-permute-start(bf16[32,1024]{1,0:T(8,128)(2,1)S(1)} %shard_map.100.refs_0_), channel_id=1, source_target_pairs={{0,16},{1,17},{2,18},{3,19},{4,20},{5,21},{6,22},{7,23},{8,24},{9,... | collective-permute-start | bytes 196616 | tf_op jit(solution)/shard_map/ppermute | solution.py:25
  89.6 6.2 %collective-permute-start.25 = (bf16[32,1024]{1,0:T(8,128)(2,1)S(1)}, bf16[32,1024]{1,0:T(8,128)(2,1)S(1)}, u32[]{:S(2)}, u32[]{:S(2)}) collective-permute-start(bf16[32,1024]{1,0:T(8,128)(2,1)S(1)} %shard_map.100.refs_0_), channel_id=1, source_target_pairs={{0,24},{1,25},{2,26},{3,27},{4,28},{5,29},{6,30},{7,31},{8,16},{9,... | collective-permute-start | bytes 196616 | tf_op jit(solution)/shard_map/ppermute | solution.py:25
  95.8 1.3 %collective-permute-start.26 = (bf16[32,1024]{1,0:T(8,128)(2,1)S(1)}, bf16[32,1024]{1,0:T(8,128)(2,1)S(1)}, u32[]{:S(2)}, u32[]{:S(2)}) collective-permute-start(bf16[32,1024]{1,0:T(8,128)(2,1)S(1)} %shard_map.101.held_ref), channel_id=1, source_target_pairs={{0,1},{1,0},{2,3},{3,2},{4,5},{5,4},{6,7},{7,6},{8,9},{9,8},{10,11... | collective-permute-start | bytes 196616 | tf_op jit(solution)/shard_map/ppermute | solution.py:25
